TPU v7x, 128 devices: a whole 4x4x4 slice. The times are simulated.
128 devices in a mesh: row: 16 (over x, y), col: 8 (over z, core).
Axes of the slice: x: 4, y: 4, z: 4, core: 2. Of those that a mesh axis runs over, the one named last changes fastest.
Arguments:
- rhs_rows: float32 [65536, 256], P(('row', 'col')), may hold values from -6 to 6
- dest_row: int32 [65536], P(('row', 'col')), may hold values from 0 to 65535, as said below
- diag_inverse: bfloat16 [4, 128, 128, 128], P(None, ('row', 'col')), may hold values from -1 to 1.5, as said below
- lower_blocks: bfloat16 [3, 16, 8, 128, 8, 16, 128], P(None, 'row', None, None, 'col'), may hold values from -0.046875 to 0.046875
- block_mask: int32 [3, 16, 8, 8, 16], P(None, 'row', None, 'col'), may hold values 0 or 1
Outputs:
- solution: bfloat16 [4, 128, 128, 256], P(None, ('row', 'col'))
Inputs may be any that keep to these rules, and one draw needn't show every extreme that they name: dest_row is a permutation of the rows. In each aligned block of 512 entries, exactly 4 entries g have (g // 128) % 128 equal to q, for every supernode index q. `diag_inverse`: every block is lower triangular with positive diagonal entries.
All inputs are finite; a program needn't handle non-finite values. No bound on the sum of `block_mask` on one device may be relied on, other than what follows from the above.
Results may differ from a plain program's by a relative error of at most 0.029.
Values may be sent and summed in bfloat16 or wider, within the bound.
A program may use at most 128 MiB of HBM per device.

v0:
```python
import jax
import jax.numpy as jnp
from jax import lax
from jax.sharding import PartitionSpec as P

B = 128
NLEV = 4


def per_device(rhs_rows, dest_row, diag_inverse, lower_blocks, block_mask):
    col_count = lax.axis_size("col")
    row_count = lax.axis_size("row")
    supernodes = row_count * col_count
    local_rows = rhs_rows.shape[0]
    column_total = rhs_rows.shape[1]
    group_rows = local_rows // supernodes
    owner_idx = dest_row // B % supernodes
    position = dest_row // (supernodes * B) * B + dest_row % B
    sort_order = jnp.argsort(owner_idx, stable=True)
    sending = rhs_rows[sort_order]
    places = position[sort_order]
    arrived, arrived_pos = (
        lax.all_to_all(
            sending.reshape(supernodes, group_rows, column_total).astype(jnp.bfloat16),
            ("row", "col"),
            split_axis=0,
            concat_axis=0,
            tiled=True,
        ).astype(jnp.float32),
        lax.all_to_all(
            places.reshape(supernodes, group_rows),
            ("row", "col"),
            split_axis=0,
            concat_axis=0,
            tiled=True,
        ),
    )
    ordered = (
        jnp.zeros_like(rhs_rows)
        .at[arrived_pos.reshape(local_rows)]
        .set(arrived.reshape(local_rows, column_total))
    )
    ordered = ordered.reshape(NLEV, B, column_total)
    diag_inv = diag_inverse[:, 0]
    masked = []
    for level_idx in range(NLEV - 1):
        block_tile = lower_blocks[level_idx, 0, :, :, 0]
        tile_mask = block_mask[level_idx, 0, :, 0, :].astype(jnp.bfloat16)
        masked.append(
            (block_tile * tile_mask[:, None, :, None]).reshape(col_count * B, row_count * B)
        )
    column_count = ordered.shape[2]
    solved = []
    for level_idx in range(NLEV):
        if level_idx == 0:
            residual = ordered[0].astype(jnp.bfloat16)
        else:
            level_tile = masked[level_idx - 1]

            def add_piece(running, shard_piece, first_row, level_tile=level_tile):
                return jnp.dot(level_tile, shard_piece, preferred_element_type=jnp.float32)

            start_sum = jnp.zeros((col_count * B, column_count), jnp.float32)
            partial_sum = add_piece(
                start_sum,
                lax.all_gather(solved[level_idx - 1], "row", axis=0, tiled=True),
                jnp.int32(0),
            )
            coupled = lax.psum_scatter(
                partial_sum.astype(jnp.bfloat16), "col", scatter_dimension=0, tiled=True
            ).astype(jnp.float32)
            residual = (ordered[level_idx] - coupled).astype(jnp.bfloat16)
        solved.append(
            jnp.dot(diag_inv[level_idx], residual, preferred_element_type=jnp.float32).astype(
                jnp.bfloat16
            )
        )
    solution = [None] * NLEV
    for level_idx in range(NLEV - 1, -1, -1):
        if level_idx == NLEV - 1:
            residual = solved[level_idx]
        else:
            upper_blocks = lax.all_gather(solution[level_idx + 1], "col", axis=0, tiled=True)
            level_tile = masked[level_idx]

            def column_term(first_row, row_span, level_tile=level_tile, upper_blocks=upper_blocks):
                return lax.dot_general(
                    level_tile,
                    upper_blocks,
                    (((0,), (0,)), ((), ())),
                    preferred_element_type=jnp.float32,
                )

            back_coupled = lax.psum_scatter(
                column_term(jnp.int32(0), B * lax.axis_size("row")).astype(jnp.bfloat16),
                "row",
                scatter_dimension=0,
                tiled=True,
            ).astype(jnp.float32)
            residual = (solved[level_idx].astype(jnp.float32) - back_coupled).astype(jnp.bfloat16)
        product = lax.dot_general(
            diag_inv[level_idx],
            residual,
            (((0,), (0,)), ((), ())),
            preferred_element_type=jnp.float32,
        )
        solution[level_idx] = product.astype(jnp.bfloat16)
    results = jnp.stack(solution)
    return results[:, None]


def solution(mesh):
    in_specs = (
        P(("row", "col"), None),
        P(("row", "col")),
        P(None, ("row", "col"), None, None),
        P(None, "row", None, None, "col", None, None),
        P(None, "row", None, "col", None),
    )
    out_specs = P(None, ("row", "col"), None, None)
    return jax.shard_map(
        per_device, mesh=mesh, in_specs=in_specs, out_specs=out_specs, check_vma=False
    )
```

profile of v0, /device:TPU:1, one launch (start us, length us, event | category | flops | bytes accessed | tf_op | source)
XLA Modules:
  0.0 586.0 jit_solution(4313193197530527790)
XLA Ops:
  7.3 3.8 sort.17
  15.3 11.5 %all-to-all-start = ((s32[128,1,4]{2,1,0:T(1,128)}), s32[128,1,4]{2,1,0:T(1,128)S(1)}, u32[]{:S(2)}, u32[]{:S(2)}) async-start(s32[128,1,4]{2,1,0:T(1,128)} %bitcast), calls=%async_computation | async-start | bytes 131072 | tf_op jit(solution)/shard_map/all_to_all | solution.py:30
  29.2 7.0 %all-to-all-done = s32[128,1,4]{2,1,0:T(1,128)S(1)} async-done(((s32[128,1,4]{2,1,0:T(1,128)}), s32[128,1,4]{2,1,0:T(1,128)S(1)}, u32[]{:S(2)}, u32[]{:S(2)}) %all-to-all-start) | async-done | bytes 2080 | tf_op jit(solution)/shard_map/all_to_all | solution.py:30
  36.2 4.8 all-to-all-start.1
  42.5 9.4 %all-to-all-done.1 = bf16[128,4,256]{2,1,0:T(4,128)(2,1)S(1)} async-done(((bf16[128,4,256]{2,1,0:T(4,128)(2,1)}), bf16[128,4,256]{2,1,0:T(4,128)(2,1)S(1)}, u32[]{:S(2)}, u32[]{:S(2)}) %all-to-all-start.1) | async-done | bytes 262176 | tf_op jit(solution)/shard_map/all_to_all | solution.py:23
  55.2 8.7 %fusion.34 = (bf16[1,1,8,128,1,16,128]{6,5,4,3,2,1,0:T(8,128)(2,1)}, bf16[1,1,8,128,1,16,128]{6,5,4,3,2,1,0:T(8,128)(2,1)}, bf16[1,1,8,128,1,16,128]{6,5,4,3,2,1,0:T(8,128)(2,1)}) fusion(bf16[3,1,8,128,1,16,128]{6,5,4,3,2,1,0:T(8,128)(2,1)} %param.8), kind=kLoop, calls=%fused_computation.74 | loop fusion | bytes 25165824 | tf_op jit(solution)/shard_map/slice | solution.py:47
  64.0 29.5 %all-gather.4.cloned.1.call-done = bf16[2048,256]{0,1:T(8,128)(2,1)} async-done(((bf16[128,256]{0,1:T(8,128)(2,1)}), bf16[2048,256]{0,1:T(8,128)(2,1)}) %all-gather.4.cloned.1.call-update) | async-done | bytes 1048592 | tf_op jit(solution)/shard_map/all_gather | solution.py:66
  97.2 3.7 convolution_convert_fusion.5
  100.9 29.1 %reduce-scatter.13.cloned.1.call-done = bf16[128,256]{1,0:T(8,128)(2,1)} async-done(((bf16[1024,256]{1,0:T(8,128)(2,1)}), bf16[128,256]{1,0:T(8,128)(2,1)}) %reduce-scatter.13.cloned.1.call-update) | async-done | bytes 65552 | tf_op jit(solution)/shard_map/reduce_scatter | solution.py:69
  131.8 44.2 %all-gather.6.cloned.1.call-done = bf16[2048,256]{0,1:T(8,128)(2,1)} async-done(((bf16[128,256]{0,1:T(8,128)(2,1)}), bf16[2048,256]{0,1:T(8,128)(2,1)}) %all-gather.6.cloned.1.call-update) | async-done | bytes 1048592 | tf_op jit(solution)/shard_map/all_gather | solution.py:66
  179.6 3.7 convolution_convert_fusion.4
  183.4 29.1 %reduce-scatter.15.cloned.1.call-done = bf16[128,256]{1,0:T(8,128)(2,1)} async-done(((bf16[1024,256]{1,0:T(8,128)(2,1)}), bf16[128,256]{1,0:T(8,128)(2,1)}) %reduce-scatter.15.cloned.1.call-update) | async-done | bytes 65552 | tf_op jit(solution)/shard_map/reduce_scatter | solution.py:69
  214.4 43.6 %all-gather.8.cloned.1.call-done = bf16[2048,256]{0,1:T(8,128)(2,1)} async-done(((bf16[128,256]{0,1:T(8,128)(2,1)}), bf16[2048,256]{0,1:T(8,128)(2,1)}) %all-gather.8.cloned.1.call-update) | async-done | bytes 1048592 | tf_op jit(solution)/shard_map/all_gather | solution.py:66
  261.7 3.7 convolution_convert_fusion.3
  265.4 29.1 %reduce-scatter.17.cloned.1.call-done = bf16[128,256]{1,0:T(8,128)(2,1)} async-done(((bf16[1024,256]{1,0:T(8,128)(2,1)}), bf16[128,256]{1,0:T(8,128)(2,1)}) %reduce-scatter.17.cloned.1.call-update) | async-done | bytes 65552 | tf_op jit(solution)/shard_map/reduce_scatter | solution.py:69
  295.6 15.7 %all_gather.21 = bf16[1024,256]{0,1:T(8,128)(2,1)S(1)} all-gather(bf16[128,256]{0,1:T(8,128)(2,1)S(1)} %bitcast.107), channel_id=1, replica_groups=mesh['row'=16,'col'=8] {'col'}, dimensions={0}, use_global_device_ids=true | all-gather | bytes 589824 | tf_op jit(solution)/shard_map/all_gather | solution.py:83
  311.3 7.7 %convolution_convert_fusion.2 = bf16[2048,256]{1,0:T(8,128)(2,1)} fusion(bf16[1024,256]{0,1:T(8,128)(2,1)S(1)} %all_gather.21, bf16[128,8,16,128]{3,2,1,0:T(8,128)(2,1)} %bitcast.100, bf16[128,8,16,128]{3,2,1,0:T(8,128)(2,1)} %bitcast.105), kind=kOutput, calls=%fused_computation.8 | convolution fusion | flops 1076363264 | bytes 9961472 | tf_op jit(solution)/shard_map/dot_general | solution.py:87
  319.0 71.8 %reduce-scatter.19.cloned.1.call-done = bf16[128,256]{1,0:T(8,128)(2,1)} async-done(((bf16[2048,256]{1,0:T(8,128)(2,1)}), bf16[128,256]{1,0:T(8,128)(2,1)}) %reduce-scatter.19.cloned.1.call-update) | async-done | bytes 65552
  391.9 15.4 %all_gather.22 = bf16[1024,256]{0,1:T(8,128)(2,1)S(1)} all-gather(bf16[128,256]{0,1:T(8,128)(2,1)S(1)} %bitcast.109), channel_id=1, replica_groups=mesh['row'=16,'col'=8] {'col'}, dimensions={0}, use_global_device_ids=true | all-gather | bytes 589824 | tf_op jit(solution)/shard_map/all_gather | solution.py:83
  407.4 7.6 %convolution_convert_fusion.1 = bf16[2048,256]{1,0:T(8,128)(2,1)} fusion(bf16[1024,256]{0,1:T(8,128)(2,1)S(1)} %all_gather.22, bf16[128,8,16,128]{3,2,1,0:T(8,128)(2,1)} %bitcast.98, bf16[128,8,16,128]{3,2,1,0:T(8,128)(2,1)} %bitcast.103), kind=kOutput, calls=%fused_computation.7 | convolution fusion | flops 1076363264 | bytes 9961472 | tf_op jit(solution)/shard_map/dot_general | solution.py:87
  415.1 68.9 %reduce-scatter.21.cloned.1.call-done = bf16[128,256]{1,0:T(8,128)(2,1)} async-done(((bf16[2048,256]{1,0:T(8,128)(2,1)}), bf16[128,256]{1,0:T(8,128)(2,1)}) %reduce-scatter.21.cloned.1.call-update) | async-done | bytes 65552
  485.1 15.7 %all_gather.23 = bf16[1024,256]{0,1:T(8,128)(2,1)S(1)} all-gather(bf16[128,256]{0,1:T(8,128)(2,1)S(1)} %bitcast.111), channel_id=1, replica_groups=mesh['row'=16,'col'=8] {'col'}, dimensions={0}, use_global_device_ids=true | all-gather | bytes 589824 | tf_op jit(solution)/shard_map/all_gather | solution.py:83
  500.8 7.7 %convolution_convert_fusion = bf16[2048,256]{1,0:T(8,128)(2,1)} fusion(bf16[1024,256]{0,1:T(8,128)(2,1)S(1)} %all_gather.23, bf16[128,8,16,128]{3,2,1,0:T(8,128)(2,1)} %bitcast.96, bf16[128,8,16,128]{3,2,1,0:T(8,128)(2,1)} %bitcast.101), kind=kOutput, calls=%fused_computation.6 | convolution fusion | flops 1076363264 | bytes 9961472 | tf_op jit(solution)/shard_map/dot_general | solution.py:87
  508.5 69.0 %reduce-scatter.23.cloned.1.call-done = bf16[128,256]{1,0:T(8,128)(2,1)} async-done(((bf16[2048,256]{1,0:T(8,128)(2,1)}), bf16[128,256]{1,0:T(8,128)(2,1)}) %reduce-scatter.23.cloned.1.call-update) | async-done | bytes 65552
  (73 shorter events, 32.4 us)
Async XLA Ops:
  6.5 20.3 %copy-start = (f32[512,256]{1,0:T(8,128)S(1)}, f32[512,256]{1,0:T(8,128)}, u32[]{:S(2)}) copy-start(f32[512,256]{1,0:T(8,128)} %param.5) | copy-start | bytes 1572868
  6.5 47.8 %copy-start.10 = (bf16[4,1,128,128]{3,2,1,0:T(8,128)(2,1)S(1)}, bf16[4,1,128,128]{3,2,1,0:T(8,128)(2,1)}, u32[]{:S(2)}) copy-start(bf16[4,1,128,128]{3,2,1,0:T(8,128)(2,1)} %param.7) | copy-start | bytes 393220
  6.5 48.7 %copy-start.11 = (s32[3,1,8,1,16]{4,3,2,1,0:T(1,128)S(1)}, s32[3,1,8,1,16]{4,3,2,1,0:T(1,128)}, u32[]{:S(2)}) copy-start(s32[3,1,8,1,16]{4,3,2,1,0:T(1,128)} %param.9) | copy-start | bytes 4612
  15.3 20.9 %all-to-all-start = ((s32[128,1,4]{2,1,0:T(1,128)}), s32[128,1,4]{2,1,0:T(1,128)S(1)}, u32[]{:S(2)}, u32[]{:S(2)}) async-start(s32[128,1,4]{2,1,0:T(1,128)} %bitcast), calls=%async_computation | async-start | bytes 131072 | tf_op jit(solution)/shard_map/all_to_all | solution.py:30
  36.2 15.7 %all-to-all-start.1 = ((bf16[128,4,256]{2,1,0:T(4,128)(2,1)}), bf16[128,4,256]{2,1,0:T(4,128)(2,1)S(1)}, u32[]{:S(2)}, u32[]{:S(2)}) async-start(bf16[128,4,256]{2,1,0:T(4,128)(2,1)} %convert_element_type.143), calls=%async_computation.1 | async-start | bytes 524288 | tf_op jit(solution)/shard_map/all_to_all | solution.py:23
  40.9 52.5 %all-gather.4.cloned.1.call-start = ((), (), s32[]{:S(2)}) async-start(), calls=%async_computation.8 | async-start | bytes 1114112 | tf_op jit(solution)/shard_map/all_gather | solution.py:66
  55.2 74.9 %reduce-scatter.13.cloned.1.call-start = ((), (), s32[]{:S(2)}) async-start(), calls=%async_computation.9 | async-start | bytes 589824 | tf_op jit(solution)/shard_map/reduce_scatter | solution.py:69
  93.5 3.7 copy-start.4
  94.1 2.1 copy-start.1
  100.9 75.0 %all-gather.6.cloned.1.call-start = ((), (), s32[]{:S(2)}) async-start(), calls=%async_computation.10 | async-start | bytes 1114112 | tf_op jit(solution)/shard_map/all_gather | solution.py:66
  131.7 80.8 %reduce-scatter.15.cloned.1.call-start = ((), (), s32[]{:S(2)}) async-start(), calls=%async_computation.11 | async-start | bytes 589824 | tf_op jit(solution)/shard_map/reduce_scatter | solution.py:69
  175.9 3.7 copy-start.5
  176.5 2.1 copy-start.2
  183.3 74.6 %all-gather.8.cloned.1.call-start = ((), (), s32[]{:S(2)}) async-start(), calls=%async_computation.12 | async-start | bytes 1114112 | tf_op jit(solution)/shard_map/all_gather | solution.py:66
  214.1 80.3 %reduce-scatter.17.cloned.1.call-start = ((), (), s32[]{:S(2)}) async-start(), calls=%async_computation.13 | async-start | bytes 589824 | tf_op jit(solution)/shard_map/reduce_scatter | solution.py:69
  258.0 3.7 copy-start.6
  258.6 2.1 copy-start.3
  265.3 125.5 %reduce-scatter.19.cloned.1.call-start = ((), (), s32[]{:S(2)}) async-start(), calls=%async_computation.14 | async-start | bytes 1114112
  311.3 80.5 %copy-start.9 = (bf16[128,256]{0,1:T(8,128)(2,1)S(1)}, bf16[128,256]{0,1:T(8,128)(2,1)}, u32[]{:S(2)}) copy-start(bf16[128,256]{0,1:T(8,128)(2,1)} %fusion.2) | copy-start | bytes 196612
  319.0 165.0 %reduce-scatter.21.cloned.1.call-start = ((), (), s32[]{:S(2)}) async-start(), calls=%async_computation.15 | async-start | bytes 1114112
  407.4 77.6 %copy-start.8 = (bf16[128,256]{0,1:T(8,128)(2,1)S(1)}, bf16[128,256]{0,1:T(8,128)(2,1)}, u32[]{:S(2)}) copy-start(bf16[128,256]{0,1:T(8,128)(2,1)} %fusion.1) | copy-start | bytes 196612
  415.0 162.5 %reduce-scatter.23.cloned.1.call-start = ((), (), s32[]{:S(2)}) async-start(), calls=%async_computation.16 | async-start | bytes 1114112
  500.8 77.7 %copy-start.7 = (bf16[128,256]{0,1:T(8,128)(2,1)S(1)}, bf16[128,256]{0,1:T(8,128)(2,1)}, u32[]{:S(2)}) copy-start(bf16[128,256]{0,1:T(8,128)(2,1)} %fusion) | copy-start | bytes 196612
Sparse Core Ops, SparseCore 0:
  55.3 38.1 all-gather.3
  101.0 28.9 reduce-scatter.12
  132.4 43.4 all-gather.5
  183.4 28.9 reduce-scatter.14
  214.4 43.4 all-gather.7
  265.5 28.9 reduce-scatter.16
  319.1 71.6 reduce-scatter.18
  415.2 68.7 reduce-scatter.20
  508.6 68.8 reduce-scatter.22
where the time goes:
time: 588 us; the launch traced here: 586 us
  waiting for transfers between devices  431 us (73%)
  blocking collectives  46.8 us (8%)
  matrix products  39.7 us (7%)
  local copies, waits for them, and re-layouts  33.2 us (6%)
  starting transfers between devices  16.8 us (3%)
  between operations  13.5 us (2%)
    unnamed x12, waiting for transfers between devices  210 us
    all_gather x3, waiting for transfers between devices, per_device(): lax.all_gather(solved[level_idx - 1], 'row', axis=0, tiled=True)  117 us
    reduce_scatter x3, waiting for transfers between devices, per_device(): lax.psum_scatter(partial_sum.astype(jnp.bfloat16), 'col', scatter_dimensi...  87.2 us
    all_gather x3, blocking collectives, per_device(): lax.all_gather(solution[level_idx + 1], 'col', axis=0, tiled=True)  46.8 us
    dot_general x3, matrix products, column_term(): lax.dot_general(level_tile, upper_blocks, (((0,), (0,)), ((), ())), prefe...  23 us
    unnamed x27, local copies, waits for them, and re-layouts  12.1 us
  transfers between devices with their start and end apart: 11, of which 11 were waited for; matrix products, arithmetic and copies ran while one was open for 2% of the time, Pallas kernels for 0%

commit v1 on v0

v1 whole, which is shorter than its diff:
```python
import functools

import jax
import jax.numpy as jnp
from jax import lax
from jax.experimental import pallas as pl
from jax.experimental.pallas import tpu as pltpu
from jax.sharding import PartitionSpec as P

B = 128
NLEV = 4
N = 256
MESH = pl.DeviceIdType.MESH
F32 = jnp.float32
BF16 = jnp.bfloat16


def dot(a, b):
    return jnp.dot(a, b, preferred_element_type=F32)


def solve_kernel(
    ordered_ref, diag_ref, mask_ref, w_hbm, out_ref,
    raw, wd, gath, acc, sib_out, sib_in, z_out, z_in, solved_t, upper, part_out, part_in, line_out, line_in,
    load_sem, ag_s, ag_r, sib_s, sib_r, z_s, z_r, up_s, up_r, fw_s, fw_r, p1_s, p1_r, p2_s, p2_r,
):
    row = lax.axis_index("row")
    col = lax.axis_index("col")
    x, y = row // 4, row % 4
    z, core = col // 2, col % 2
    other = 1 - core

    def row_of(h, u, v):
        return (u % 4) * 4 + v % 4 if h == 0 else (v % 4) * 4 + u % 4

    first = (x, y)
    second = (y, x)

    def remote(src, dst, ssem, rsem, dev):
        return pltpu.make_async_remote_copy(
            src_ref=src, dst_ref=dst, send_sem=ssem, recv_sem=rsem, device_id=dev, device_id_type=MESH
        )

    sibling = (row, z * 2 + other)

    def z_peer(d):
        return (row, ((z + d) % 4) * 2 + core)

    barrier = pltpu.get_barrier_semaphore()
    peers = [sibling] + [z_peer(d) for d in (1, 2, 3)]
    peers += [(row_of(0, x + d, y), col) for d in (1, 2, 3)]
    peers += [(row_of(0, x, y + d), col) for d in (1, 2, 3)]
    for dev in peers:
        pl.semaphore_signal(barrier, inc=1, device_id=dev, device_id_type=MESH)

    loads = [pltpu.make_async_copy(w_hbm.at[l, 0, :, :, 0], raw.at[l], load_sem.at[l]) for l in range(3)]
    for load in loads:
        load.start()

    out_row = lax.broadcasted_iota(jnp.int32, (256, 256), 0)
    in_row = lax.broadcasted_iota(jnp.int32, (256, 256), 1)
    perm = jnp.where(in_row == (out_row % 16) * 16 + out_row // 16, 1.0, 0.0).astype(BF16)

    def relayout(l):
        def one(i, carry):
            zz, cc = i // 2, i % 2
            scale = [mask_ref[l, i * 16 + p].astype(F32) for p in range(16)]
            for k0 in range(0, 8, 2):
                piece = jnp.concatenate(
                    [raw[l, i, (k0 + s) * 16:(k0 + s + 1) * 16].reshape(256, B) for s in range(2)], axis=1
                )
                moved = dot(perm, piece)
                for p in range(16):
                    for s in range(2):
                        tile = moved[p * 16:(p + 1) * 16, s * B:(s + 1) * B] * scale[p]
                        wd[l, p, cc, zz, (k0 + s) * 16:(k0 + s + 1) * 16, :] = tile.astype(BF16)
            return carry

        lax.fori_loop(0, 8, one, 0)

    def put_solved(l, residual):
        solved = dot(diag_ref[l], residual).astype(BF16)
        return solved

    level0 = put_solved(0, ordered_ref[0].astype(BF16))
    gath[0, 0, row] = level0[:, :B]
    gath[0, 1, row] = level0[:, B:]
    solved_t[0] = level0.astype(F32).T
    pl.semaphore_wait(barrier, len(peers))

    def gather_copy(l, h, slot, idx, dev):
        return remote(gath.at[l, h, slot], gath.at[l, h, slot], ag_s.at[l, h, idx], ag_r.at[l, h, idx], dev)

    def pair_rhs(l, p):
        return jnp.concatenate([gath[l, 0, p], gath[l, 1, p]], axis=1)

    def down(l, carry):
        for h in range(2):
            u, v = first if h == 0 else second
            for d in (2, 1, 3):
                gather_copy(l, h, row, d - 1, (row_of(h, u + d, v), col)).start()
        for e in (0, 1, 3, 2):
            for h in range(2):
                u, v = first if h == 0 else second
                slot = row_of(h, u - e, v)
                if e:
                    gather_copy(l, h, slot, e - 1, (row, col)).wait_recv()
                for d in (2, 1, 3):
                    gather_copy(l, h, slot, 3 + e * 3 + d - 1, (row_of(h, u, v + d), col)).start()
            if e == 0:
                loads_wait(l)
                relayout(l)
        order = [(a, b) for a in (0, 1, 3) for b in (0, 1, 3)] + [(a, b) for a in range(4) for b in range(4) if 2 in (a, b)]
        done = set()

        def arrive(a, b):
            for h in range(2):
                e, d = (a, b) if h == 0 else (b, a)
                u, v = first if h == 0 else second
                if d and (h, e, d) not in done:
                    done.add((h, e, d))
                    gather_copy(l, h, row_of(h, u - e, v - d), 3 + e * 3 + d - 1, (row, col)).wait_recv()

        def operands(some):
            slots = [row_of(0, x - a, y - b) for a, b in some]
            rhs = jnp.concatenate([pair_rhs(l, p) for p in slots], axis=0)
            return slots, rhs

        def lhs(slots, c, r, n):
            return jnp.concatenate([wd[l, p, c, r:r + n].reshape(n * B, B) for p in slots], axis=1)

        for a, b in order[:8]:
            arrive(a, b)
        slots, rhs = operands(order[:8])
        for c in range(2):
            for r in range(0, 4, 2):
                acc[c, r:r + 2] = dot(lhs(slots, c, r, 2), rhs).reshape(2, B, N)
        for a, b in order[8:]:
            arrive(a, b)
        slots, rhs = operands(order[8:])
        for step, c in enumerate((other, core)):
            for half in range(2):
                r = ((z // 2 + 1 - half) % 2) * 2
                left = jnp.concatenate([wd[l, p, c, pl.ds(r, 2)].reshape(2 * B, B) for p in slots], axis=1)
                total = acc[c, pl.ds(r, 2)] + dot(left, rhs).reshape(2, B, N)
                if step == 0:
                    sib_out[l, pl.ds(r, 2)] = total.astype(BF16)
                    for s in range(2):
                        remote(sib_out.at[l, r + s], sib_in.at[l, r + s], sib_s.at[l, half * 2 + s], sib_r.at[l, r + s], sibling).start()
                else:
                    acc[c, pl.ds(r, 2)] = total
        for d in (2, 1, 3, 0):
            zz = (z + d) % 4
            remote(sib_out.at[l, zz], sib_in.at[l, zz], sib_s.at[l, 0], sib_r.at[l, zz], sibling).wait_recv()
            total = acc[core, zz] + sib_in[l, zz].astype(F32)
            if d:
                z_out[l, d - 1] = total.astype(BF16)
                remote(z_out.at[l, d - 1], z_in.at[l, d - 1], z_s.at[l, d - 1], z_r.at[l, d - 1], z_peer(d)).start()
            else:
                own = total
        for d in (1, 3, 2):
            remote(z_out.at[l, d - 1], z_in.at[l, d - 1], z_s.at[l, d - 1], z_r.at[l, d - 1], z_peer(d)).wait_recv()
            own = own + z_in[l, d - 1].astype(F32)
        residual = (ordered_ref[l + 1] - own).astype(BF16)
        solved = put_solved(l + 1, residual)
        gath[l + 1, 0, row] = solved[:, :B]
        gath[l + 1, 1, row] = solved[:, B:]
        solved_t[l + 1] = solved.astype(F32).T
        return carry

    def loads_wait(l):
        pltpu.make_async_copy(w_hbm.at[l, 0, :, :, 0], raw.at[l], load_sem.at[l]).wait()

    lax.fori_loop(0, 3, down, 0)

    def finish(l, slot, residual_t):
        sol_t = dot(residual_t.astype(BF16), diag_ref[l]).astype(BF16)
        upper[slot, core, z] = sol_t
        return sol_t

    top = finish(3, 0, solved_t[3])
    out_ref[3] = top.astype(F32).T.astype(BF16)

    def up_copy(t, d):
        return remote(upper.at[t, core, z], upper.at[t, core, z], up_s.at[t, d - 1], up_r.at[t, d - 1], z_peer(d))

    def forward_copy(t, d):
        slot = upper.at[t, core, (z - d) % 4]
        return remote(slot, slot, fw_s.at[t, d], fw_r.at[t, d], sibling)

    def part_copy(t, h, du, dv):
        u, v = first if h == 0 else second
        return remote(
            part_out.at[t, h, du, dv], part_in.at[t, h, du, dv],
            p1_s.at[t, h, du, dv], p1_r.at[t, h, du, dv], (row_of(h, u + du, v), col),
        )

    def line_copy(t, h, dv):
        u, v = first if h == 0 else second
        return remote(
            line_out.at[t, h, dv], line_in.at[t, h, dv], p2_s.at[t, h, dv], p2_r.at[t, h, dv], (row_of(h, u, v + dv), col)
        )

    def up(t, carry):
        l = 2 - t
        for d in (2, 1, 3):
            up_copy(t, d).start()
        forward_copy(t, 0).start()
        for d in (1, 3, 2):
            slot = upper.at[t, core, (z - d) % 4]
            remote(slot, slot, up_s.at[t, d - 1], up_r.at[t, d - 1], sibling).wait_recv()
            forward_copy(t, d).start()
        for d in (0, 1, 3, 2):
            slot = upper.at[t, other, (z - d) % 4]
            remote(slot, slot, fw_s.at[t, d], fw_r.at[t, d], sibling).wait_recv()
        left = jnp.concatenate([upper[t, c, r] for c in range(2) for r in range(4)], axis=1)
        pairs = [((2, 2), (2, 1)), ((2, 3), (2, 0)), ((1, 2), (3, 2)), ((0, 2), (1, 1)),
                 ((1, 3), (3, 1)), ((3, 3), (1, 0)), ((3, 0), (0, 1)), ((0, 3), (0, 0))]
        for two in pairs:
            slots = [row_of(0, x + a, y + b) for a, b in two]
            right = jnp.concatenate([wd[l, p].reshape(8 * B, B) for p in slots], axis=1)
            value = dot(left, right).astype(BF16)
            for s, (a, b) in enumerate(two):
                for h in range(2):
                    du, dv = (a, b) if h == 0 else (b, a)
                    part_out[t, h, du, dv] = value[h * B:(h + 1) * B, s * B:(s + 1) * B]
                    if du:
                        part_copy(t, h, du, dv).start()
        keep = []
        for dv in (2, 1, 3, 0):
            for h in range(2):
                total = part_out[t, h, 0, dv].astype(F32)
                for du in (1, 3, 2):
                    part_copy(t, h, du, dv).wait_recv()
                    total = total + part_in[t, h, du, dv].astype(F32)
                if dv:
                    line_out[t, h, dv] = total.astype(BF16)
                    line_copy(t, h, dv).start()
                else:
                    keep.append(total)
        for h in range(2):
            for dv in (1, 3, 2):
                line_copy(t, h, dv).wait_recv()
                keep[h] = keep[h] + line_in[t, h, dv].astype(F32)
        residual_t = solved_t[l] - jnp.concatenate(keep, axis=0)
        sol_t = finish(l, t + 1, residual_t)
        out_ref[l] = sol_t.astype(F32).T.astype(BF16)
        return carry

    lax.fori_loop(0, 3, up, 0)

    def drain(l, carry):
        for h in range(2):
            for idx in range(15):
                gather_copy(l, h, row, idx, (row, col)).wait_send()
            for du in range(1, 4):
                for dv in range(4):
                    part_copy(l, h, du, dv).wait_send()
            for dv in range(1, 4):
                line_copy(l, h, dv).wait_send()
        for s in range(4):
            remote(sib_out.at[l, s], sib_in.at[l, s], sib_s.at[l, s], sib_r.at[l, s], sibling).wait_send()
            forward_copy(l, s).wait_send()
        for d in range(1, 4):
            remote(z_out.at[l, d - 1], z_in.at[l, d - 1], z_s.at[l, d - 1], z_r.at[l, d - 1], z_peer(d)).wait_send()
            up_copy(l, d).wait_send()
        return carry

    lax.fori_loop(0, 3, drain, 0)


def solve(ordered, diag, mask, lower):
    vmem = pl.BlockSpec(memory_space=pltpu.VMEM)
    dma = pltpu.SemaphoreType.DMA
    return pl.pallas_call(
        solve_kernel,
        out_shape=jax.ShapeDtypeStruct((NLEV, B, N), BF16),
        in_specs=[vmem, vmem, pl.BlockSpec(memory_space=pltpu.SMEM), pl.BlockSpec(memory_space=pl.ANY)],
        out_specs=vmem,
        scratch_shapes=[
            pltpu.VMEM((3, 8, B, 16, B), BF16),
            pltpu.VMEM((3, 16, 2, 4, B, B), BF16),
            pltpu.VMEM((4, 2, 16, B, B), BF16),
            pltpu.VMEM((2, 4, B, N), F32),
            pltpu.VMEM((3, 4, B, N), BF16),
            pltpu.VMEM((3, 4, B, N), BF16),
            pltpu.VMEM((3, 3, B, N), BF16),
            pltpu.VMEM((3, 3, B, N), BF16),
            pltpu.VMEM((4, N, B), F32),
            pltpu.VMEM((4, 2, 4, N, B), BF16),
            pltpu.VMEM((3, 2, 4, 4, B, B), BF16),
            pltpu.VMEM((3, 2, 4, 4, B, B), BF16),
            pltpu.VMEM((3, 2, 4, B, B), BF16),
            pltpu.VMEM((3, 2, 4, B, B), BF16),
            dma((3,)), dma((3, 2, 15)), dma((3, 2, 15)), dma((3, 4)), dma((3, 4)), dma((3, 3)), dma((3, 3)),
            dma((3, 3)), dma((3, 3)), dma((3, 4)), dma((3, 4)),
            dma((3, 2, 4, 4)), dma((3, 2, 4, 4)), dma((3, 2, 4)), dma((3, 2, 4)),
        ],
        compiler_params=pltpu.CompilerParams(
            collective_id=0, has_side_effects=True, vmem_limit_bytes=60 * 1024 * 1024
        ),
    )(ordered, diag, mask, lower)


def per_device(rhs_rows, dest_row, diag_inverse, lower_blocks, block_mask):
    supernodes = 128
    local_rows, column_total = rhs_rows.shape
    group_rows = local_rows // supernodes
    owner_idx = dest_row // B % supernodes
    position = dest_row // (supernodes * B) * B + dest_row % B
    sort_order = jnp.argsort(owner_idx, stable=True)
    sending = rhs_rows[sort_order]
    places = position[sort_order]
    axes = ("row", "col")
    arrived = lax.all_to_all(
        sending.reshape(supernodes, group_rows, column_total).astype(BF16), axes, split_axis=0, concat_axis=0, tiled=True
    ).astype(F32)
    arrived_pos = lax.all_to_all(places.reshape(supernodes, group_rows), axes, split_axis=0, concat_axis=0, tiled=True)
    ordered = (
        jnp.zeros_like(rhs_rows).at[arrived_pos.reshape(local_rows)].set(arrived.reshape(local_rows, column_total))
    )
    ordered = ordered.reshape(NLEV, B, column_total)
    mask = block_mask.reshape(3, 128)
    return solve(ordered, diag_inverse[:, 0], mask, lower_blocks)[:, None]


def solution(mesh):
    in_specs = (
        P(("row", "col"), None),
        P(("row", "col")),
        P(None, ("row", "col"), None, None),
        P(None, "row", None, None, "col", None, None),
        P(None, "row", None, "col", None),
    )
    out_specs = P(None, ("row", "col"), None, None)
    return jax.shard_map(per_device, mesh=mesh, in_specs=in_specs, out_specs=out_specs, check_vma=False)
```

time: 588 us -> 162 us (0.28)
  waiting for transfers between devices: 431 us -> 14.3 us
  Pallas kernels: 0 us -> 112 us
  blocking collectives: 46.8 us -> 0 us
  matrix products: 39.7 us -> 0 us
  local copies, waits for them, and re-layouts: 33.2 us -> 12.6 us
  between operations: 13.5 us -> 0.08 us
    unnamed x12 -> x0, waiting for transfers between devices: 210 us -> none
    all_gather x3 -> x0, waiting for transfers between devices: 117 us -> none  [per_device(): lax.all_gather(solved[level_idx - 1], 'row', axis=0, tiled=True)]
    pallas_call x0 -> x1, Pallas kernels: none -> 112 us  [solve(): pl.pallas_call(solve_kernel, out_shape=jax.ShapeDtypeStruct((NLEV, B, N),...]
    reduce_scatter x3 -> x0, waiting for transfers between devices: 87.2 us -> none  [per_device(): lax.psum_scatter(partial_sum.astype(jnp.bfloat16), 'col', scatter_dimensi...]
    all_gather x3 -> x0, blocking collectives: 46.8 us -> none  [per_device(): lax.all_gather(solution[level_idx + 1], 'col', axis=0, tiled=True)]
    dot_general x13 -> x0, matrix products: 39.7 us -> none  [the longest x3 23 us: column_term(): lax.dot_general(level_tile, upper_blocks, (((0,), (0,)), ((), ())), prefe...]
    unnamed x27 -> x3, local copies, waits for them, and re-layouts: 12.1 us -> 1.67 us
    slice x1 -> x0, local copies, waits for them, and re-layouts: 8.75 us -> none  [per_device(): block_tile = lower_blocks[level_idx, 0, :, :, 0]]
  transfers between devices with their start and end apart: 11 -> 2, of which waited for: 11 -> 2; matrix products, arithmetic and copies ran while one was open for 2% -> 4% of each run, Pallas kernels for 0% -> 0%
where the time goes in v1:
time: 162 us
  Pallas kernels  112 us (69%)
  starting transfers between devices  16.3 us (10%)
  waiting for transfers between devices  14.3 us (9%)
  local copies, waits for them, and re-layouts  12.6 us (8%)
  other arithmetic  6.82 us (4%)
    pallas_call x1, Pallas kernels, solve(): pl.pallas_call(solve_kernel, out_shape=jax.ShapeDtypeStruct((NLEV, B, N),...  112 us
    all_to_all x1, starting transfers between devices, per_device(): lax.all_to_all(places.reshape(supernodes, group_rows), axes, split_axis=0...  11.5 us
    all_to_all x1, waiting for transfers between devices, per_device(): lax.all_to_all(sending.reshape(supernodes, group_rows, column_total).asty...  7.26 us
    all_to_all x1, waiting for transfers between devices, per_device(): lax.all_to_all(places.reshape(supernodes, group_rows), axes, split_axis=0...  7.01 us
    all_to_all x1, starting transfers between devices, per_device(): lax.all_to_all(sending.reshape(supernodes, group_rows, column_total).asty...  4.76 us
    sort x1, other arithmetic, per_device(): sort_order = jnp.argsort(owner_idx, stable=True)  3.77 us
    gather x1, local copies, waits for them, and re-layouts, per_device(): places = position[sort_order]  3.49 us
  transfers between devices with their start and end apart: 2, of which 2 were waited for; matrix products, arithmetic and copies ran while one was open for 4% of the time, Pallas kernels for 0%

profile of v1, /device:TPU:1, one launch (start us, length us, event | category | flops | bytes accessed | tf_op | source)
XLA Modules:
  0.0 162.2 jit_solution(8986437670344846451)
XLA Ops:
  0.0 0.0 copy-start
  0.0 0.8 add_select_fusion
  0.8 3.8 %sort.17 = (s32[512]{0:T(512)}, s32[512]{0:T(512)S(1)}) sort(s32[512]{0:T(512)S(1)} %get-tuple-element.7, s32[512]{0:T(512)S(1)} %iota.4), dimensions={0}, to_apply=%region_0.1 | sort | flops 4608 | bytes 8192 | tf_op jit(solution)/shard_map/jit(argsort)/sort | solution.py:311
  4.5 3.5 %gather_fusion = s32[512]{0:T(512)S(1)} fusion(s32[512]{0:T(512)S(1)} %get-tuple-element.8, s32[1024]{0:T(1024)S(1)} %pad_clamp_fusion), kind=kCustom, calls=%fused_computation | custom fusion | bytes 6144 | tf_op jit(solution)/shard_map/gather | solution.py:313
  8.0 0.7 all_to_all.9
  8.8 11.5 %all-to-all-start = ((s32[128,1,4]{2,1,0:T(1,128)}), s32[128,1,4]{2,1,0:T(1,128)S(1)}, u32[]{:S(2)}, u32[]{:S(2)}) async-start(s32[128,1,4]{2,1,0:T(1,128)} %bitcast), calls=%async_computation | async-start | bytes 131072 | tf_op jit(solution)/shard_map/all_to_all | solution.py:318
  20.3 0.0 copy-done
  20.3 1.6 gather_fusion.1
  21.9 0.8 convert_element_type.8
  22.6 7.0 %all-to-all-done = s32[128,1,4]{2,1,0:T(1,128)S(1)} async-done(((s32[128,1,4]{2,1,0:T(1,128)}), s32[128,1,4]{2,1,0:T(1,128)S(1)}, u32[]{:S(2)}, u32[]{:S(2)}) %all-to-all-start) | async-done | bytes 2080 | tf_op jit(solution)/shard_map/all_to_all | solution.py:318
  29.6 4.8 %all-to-all-start.1 = ((bf16[128,4,256]{2,1,0:T(4,128)(2,1)}), bf16[128,4,256]{2,1,0:T(4,128)(2,1)S(1)}, u32[]{:S(2)}, u32[]{:S(2)}) async-start(bf16[128,4,256]{2,1,0:T(4,128)(2,1)} %convert_element_type.8), calls=%async_computation.1 | async-start | bytes 524288 | tf_op jit(solution)/shard_map/all_to_all | solution.py:315
  34.4 0.6 broadcast.59
  35.0 1.4 reduce.7
  36.4 0.7 reshape.54.mask_ref
  37.1 0.8 reduce.6
  38.0 0.1 reshape.50
  38.1 7.3 %all-to-all-done.1 = bf16[128,4,256]{2,1,0:T(4,128)(2,1)S(1)} async-done(((bf16[128,4,256]{2,1,0:T(4,128)(2,1)}), bf16[128,4,256]{2,1,0:T(4,128)(2,1)S(1)}, u32[]{:S(2)}, u32[]{:S(2)}) %all-to-all-start.1) | async-done | bytes 262176 | tf_op jit(solution)/shard_map/all_to_all | solution.py:315
  45.4 3.0 %scatter_custom_fusion = f32[512,256]{1,0:T(8,128)} fusion(s32[512]{0:T(512)S(1)} %bitcast.10, f32[512,256]{1,0:T(8,128)S(1)} %reshape.77, f32[]{:T(128)} %constant.40.clone.1), kind=kCustom, calls=%fused_computation.3 | custom fusion | bytes 524292 | tf_op jit(solution)/shard_map/scatter | solution.py:320
  48.4 112.1 %shard_map.55 = bf16[4,128,256]{2,1,0:T(8,128)(2,1)} custom-call(f32[4,128,256]{2,1,0:T(8,128)} %bitcast.7, bf16[4,128,128]{2,1,0:T(8,128)(2,1)} %bitcast.9, s32[3,128]{1,0:T(4,128)} %reshape.54.mask_ref, bf16[3,1,8,128,1,16,128]{6,5,4,3,2,1,0:T(8,128)(2,1)} %w_hbm.1), custom_call_target="tpu_custom_call" | custom-call | tf_op jit(solution)/shard_map/pallas_call | solution.py:275
  160.5 1.7 %copy.11 = bf16[4,1,128,256]{3,2,1,0:T(8,128)(2,1)} copy(bf16[4,1,128,256]{3,2,1,0:T(8,128)(2,1)} %bitcast.8) | data formatting | bytes 524288
  (5 shorter events, 0.1 us)
Async XLA Ops:
  0.0 20.3 %copy-start = (f32[512,256]{1,0:T(8,128)S(1)}, f32[512,256]{1,0:T(8,128)}, u32[]{:S(2)}) copy-start(f32[512,256]{1,0:T(8,128)} %param.5) | copy-start | bytes 1572868
  8.8 20.9 %all-to-all-start = ((s32[128,1,4]{2,1,0:T(1,128)}), s32[128,1,4]{2,1,0:T(1,128)S(1)}, u32[]{:S(2)}, u32[]{:S(2)}) async-start(s32[128,1,4]{2,1,0:T(1,128)} %bitcast), calls=%async_computation | async-start | bytes 131072 | tf_op jit(solution)/shard_map/all_to_all | solution.py:318
  29.6 15.7 %all-to-all-start.1 = ((bf16[128,4,256]{2,1,0:T(4,128)(2,1)}), bf16[128,4,256]{2,1,0:T(4,128)(2,1)S(1)}, u32[]{:S(2)}, u32[]{:S(2)}) async-start(bf16[128,4,256]{2,1,0:T(4,128)(2,1)} %convert_element_type.8), calls=%async_computation.1 | async-start | bytes 524288 | tf_op jit(solution)/shard_map/all_to_all | solution.py:315

commit v2 on v1

--- a/solution.py
+++ b/solution.py
@@ -1,5 +1,3 @@
-import functools
-
 import jax
 import jax.numpy as jnp
 from jax import lax
@@ -19,10 +17,22 @@
     return jnp.dot(a, b, preferred_element_type=F32)
 
 
+def dot_rows(a, b):
+    return lax.dot_general(a, b, (((1,), (1,)), ((), ())), preferred_element_type=F32)
+
+
+def one_hot(condition):
+    return jnp.where(condition, 1.0, 0.0).astype(BF16)
+
+
+def iota(shape, axis):
+    return lax.broadcasted_iota(jnp.int32, shape, axis)
+
+
 def solve_kernel(
-    ordered_ref, diag_ref, mask_ref, w_hbm, out_ref,
-    raw, wd, gath, acc, sib_out, sib_in, z_out, z_in, solved_t, upper, part_out, part_in, line_out, line_in,
-    load_sem, ag_s, ag_r, sib_s, sib_r, z_s, z_r, up_s, up_r, fw_s, fw_r, p1_s, p1_r, p2_s, p2_r,
+    rhs_ref, dest_ref, diag_ref, mask_ref, w_hbm, out_ref,
+    rows_out, rows_in, meta_out, meta_in, meta_sib, mix_out, mix_in, ordered_ref, raw, wd, gath, acc, sib_out, sib_in, z_out, z_in, solved_t, upper, part_out, part_in, line_out, line_in,
+    rows_s, rows_r, meta_s, meta_r, mix_s, mix_r, load_sem, ag_s, ag_r, sib_s, sib_r, z_s, z_r, up_s, up_r, fw_s, fw_r, p1_s, p1_r, p2_s, p2_r,
 ):
     row = lax.axis_index("row")
     col = lax.axis_index("col")
@@ -46,25 +56,35 @@
     def z_peer(d):
         return (row, ((z + d) % 4) * 2 + core)
 
+    chip = row * 4 + z
+
+    def chip_peer(k):
+        t = (chip + k) % 64
+        return t, (t // 4, (t % 4) * 2 + core)
+
     barrier = pltpu.get_barrier_semaphore()
-    peers = [sibling] + [z_peer(d) for d in (1, 2, 3)]
-    peers += [(row_of(0, x + d, y), col) for d in (1, 2, 3)]
-    peers += [(row_of(0, x, y + d), col) for d in (1, 2, 3)]
-    for dev in peers:
-        pl.semaphore_signal(barrier, inc=1, device_id=dev, device_id_type=MESH)
+    pl.semaphore_signal(barrier, inc=1, device_id=sibling, device_id_type=MESH)
+
+    def greet(k, carry):
+        pl.semaphore_signal(barrier, inc=1, device_id=chip_peer(k)[1], device_id_type=MESH)
+        return carry
+
+    lax.fori_loop(1, 64, greet, 0)
 
     loads = [pltpu.make_async_copy(w_hbm.at[l, 0, :, :, 0], raw.at[l], load_sem.at[l]) for l in range(3)]
     for load in loads:
         load.start()
 
-    out_row = lax.broadcasted_iota(jnp.int32, (256, 256), 0)
-    in_row = lax.broadcasted_iota(jnp.int32, (256, 256), 1)
-    perm = jnp.where(in_row == (out_row % 16) * 16 + out_row // 16, 1.0, 0.0).astype(BF16)
+    def loads_wait(l):
+        pltpu.make_async_copy(w_hbm.at[l, 0, :, :, 0], raw.at[l], load_sem.at[l]).wait()
+
+    out_row, in_row = iota((256, 256), 0), iota((256, 256), 1)
+    perm = one_hot(in_row == (out_row & 15) * 16 + (out_row >> 4))
 
     def relayout(l):
         def one(i, carry):
             zz, cc = i // 2, i % 2
-            scale = [mask_ref[l, i * 16 + p].astype(F32) for p in range(16)]
+            scale = [mask_ref[l, 0, i, 0, p].astype(F32) for p in range(16)]
             for k0 in range(0, 8, 2):
                 piece = jnp.concatenate(
                     [raw[l, i, (k0 + s) * 16:(k0 + s + 1) * 16].reshape(256, B) for s in range(2)], axis=1
@@ -82,11 +102,76 @@
         solved = dot(diag_ref[l], residual).astype(BF16)
         return solved
 
+    dest = dest_ref[...]
+    owner = (dest >> 7) & 127
+    place = (dest >> 14) * B + (dest & 127)
+    owned = one_hot(iota((128, 512), 0) == owner)
+    before = dot(owned, one_hot(iota((512, 512), 0) < iota((512, 512), 1)))
+    rank = jnp.sum(owned.astype(F32) * before, axis=0, keepdims=True)
+    slot = owner * 4 + rank.astype(jnp.int32)
+    sort = one_hot(iota((512, 512), 0) == slot)
+    rows_out[...] = dot(sort, rhs_ref[...].astype(BF16)).astype(BF16).reshape(64, 8, N)
+    lane = iota((128, 512), 0)
+    digit = jnp.where(lane < 8, place >> 4, place & 15)
+    digit = jnp.where((lane < 16) & ((lane & 7) == (slot & 7)), digit, 0).astype(F32).astype(BF16)
+    meta_out[...] = dot_rows(one_hot(iota((64, 512), 0) == (slot >> 3)), digit).reshape(64, 1, B)
+
+    def rows_copy(t, dev):
+        return remote(rows_out.at[t], rows_in.at[chip], rows_s, rows_r, dev)
+
+    def meta_copy(t, dev):
+        return remote(meta_out.at[t], meta_in.at[chip], meta_s, meta_r, dev)
+
+    pl.semaphore_wait(barrier, 64)
+
+    def send_rows(k, carry):
+        t, dev = chip_peer(k)
+        meta_copy(t, dev).start()
+        rows_copy(t, dev).start()
+        return carry
+
+    lax.fori_loop(1, 64, send_rows, 0)
+    rows_in[chip] = rows_out[chip]
+    meta_in[chip] = meta_out[chip]
+
+    def prepare(l, carry):
+        loads_wait(l)
+        relayout(l)
+        return carry
+
+    lax.fori_loop(0, 3, prepare, 0)
+
+    some = pl.ds(0, 63)
+    all_rows = remote(rows_out.at[some], rows_in.at[some], rows_s, rows_r, sibling)
+    all_meta = remote(meta_out.at[some], meta_in.at[some], meta_s, meta_r, sibling)
+    all_meta.wait_recv()
+    meta_swap = remote(meta_in, meta_sib, mix_s.at[0], mix_r.at[0], sibling)
+    meta_swap.start()
+    all_rows.wait_recv()
+    to, at = iota((512, 512), 0), iota((512, 512), 1)
+    half = jnp.where(to < 256, core, other)
+    mixed = dot(one_hot(at == (to & 63) * 8 + half * 4 + ((to >> 6) & 3)), rows_in[...].reshape(512, N)).astype(BF16)
+    mix_out[...] = mixed[256:]
+    mix_swap = remote(mix_out, mix_in, mix_s.at[1], mix_r.at[1], sibling)
+    mix_swap.start()
+
+    def place_rows(meta, rows):
+        digits = jnp.concatenate([meta.reshape(64, B)] * 4, axis=0)
+        at_lane, k = iota((256, B), 1), iota((256, B), 0) >> 6
+        mine = (at_lane < 16) & ((at_lane & 7) == core * 4 + k)
+        weight = jnp.where(iota((8, B), 1) < 8, 16.0, 1.0).astype(BF16)
+        where = dot_rows(weight, jnp.where(mine, digits, 0.0).astype(BF16))[:1]
+        return dot(one_hot(iota((512, 256), 0) == where.astype(jnp.int32)), rows)
+
+    total = place_rows(meta_in[...], mixed[:256])
+    meta_swap.wait_recv()
+    mix_swap.wait_recv()
+    ordered_ref[...] = (total + place_rows(meta_sib[...], mix_in[...])).reshape(NLEV, B, N)
+
     level0 = put_solved(0, ordered_ref[0].astype(BF16))
     gath[0, 0, row] = level0[:, :B]
     gath[0, 1, row] = level0[:, B:]
     solved_t[0] = level0.astype(F32).T
-    pl.semaphore_wait(barrier, len(peers))
 
     def gather_copy(l, h, slot, idx, dev):
         return remote(gath.at[l, h, slot], gath.at[l, h, slot], ag_s.at[l, h, idx], ag_r.at[l, h, idx], dev)
@@ -107,9 +192,6 @@
                     gather_copy(l, h, slot, e - 1, (row, col)).wait_recv()
                 for d in (2, 1, 3):
                     gather_copy(l, h, slot, 3 + e * 3 + d - 1, (row_of(h, u, v + d), col)).start()
-            if e == 0:
-                loads_wait(l)
-                relayout(l)
         order = [(a, b) for a in (0, 1, 3) for b in (0, 1, 3)] + [(a, b) for a in range(4) for b in range(4) if 2 in (a, b)]
         done = set()
 
@@ -167,9 +249,6 @@
         gath[l + 1, 1, row] = solved[:, B:]
         solved_t[l + 1] = solved.astype(F32).T
         return carry
-
-    def loads_wait(l):
-        pltpu.make_async_copy(w_hbm.at[l, 0, :, :, 0], raw.at[l], load_sem.at[l]).wait()
 
     lax.fori_loop(0, 3, down, 0)
 
@@ -267,17 +346,29 @@
         return carry
 
     lax.fori_loop(0, 3, drain, 0)
-
-
-def solve(ordered, diag, mask, lower):
+    all_rows.wait_send()
+    all_meta.wait_send()
+    meta_swap.wait_send()
+    mix_swap.wait_send()
+
+
+def solve(rhs, dest, diag, mask, lower):
     vmem = pl.BlockSpec(memory_space=pltpu.VMEM)
     dma = pltpu.SemaphoreType.DMA
     return pl.pallas_call(
         solve_kernel,
         out_shape=jax.ShapeDtypeStruct((NLEV, B, N), BF16),
-        in_specs=[vmem, vmem, pl.BlockSpec(memory_space=pltpu.SMEM), pl.BlockSpec(memory_space=pl.ANY)],
+        in_specs=[vmem, vmem, vmem, pl.BlockSpec(memory_space=pltpu.SMEM), pl.BlockSpec(memory_space=pl.ANY)],
         out_specs=vmem,
         scratch_shapes=[
+            pltpu.VMEM((64, 8, N), BF16),
+            pltpu.VMEM((64, 8, N), BF16),
+            pltpu.VMEM((64, 1, B), F32),
+            pltpu.VMEM((64, 1, B), F32),
+            pltpu.VMEM((64, 1, B), F32),
+            pltpu.VMEM((256, N), BF16),
+            pltpu.VMEM((256, N), BF16),
+            pltpu.VMEM((NLEV, B, N), F32),
             pltpu.VMEM((3, 8, B, 16, B), BF16),
             pltpu.VMEM((3, 16, 2, 4, B, B), BF16),
             pltpu.VMEM((4, 2, 16, B, B), BF16),
@@ -292,6 +383,7 @@
             pltpu.VMEM((3, 2, 4, 4, B, B), BF16),
             pltpu.VMEM((3, 2, 4, B, B), BF16),
             pltpu.VMEM((3, 2, 4, B, B), BF16),
+            dma, dma, dma, dma, dma((2,)), dma((2,)),
             dma((3,)), dma((3, 2, 15)), dma((3, 2, 15)), dma((3, 4)), dma((3, 4)), dma((3, 3)), dma((3, 3)),
             dma((3, 3)), dma((3, 3)), dma((3, 4)), dma((3, 4)),
             dma((3, 2, 4, 4)), dma((3, 2, 4, 4)), dma((3, 2, 4)), dma((3, 2, 4)),
@@ -299,29 +391,12 @@
         compiler_params=pltpu.CompilerParams(
             collective_id=0, has_side_effects=True, vmem_limit_bytes=60 * 1024 * 1024
         ),
-    )(ordered, diag, mask, lower)
+    )(rhs, dest, diag, mask, lower)
 
 
 def per_device(rhs_rows, dest_row, diag_inverse, lower_blocks, block_mask):
-    supernodes = 128
-    local_rows, column_total = rhs_rows.shape
-    group_rows = local_rows // supernodes
-    owner_idx = dest_row // B % supernodes
-    position = dest_row // (supernodes * B) * B + dest_row % B
-    sort_order = jnp.argsort(owner_idx, stable=True)
-    sending = rhs_rows[sort_order]
-    places = position[sort_order]
-    axes = ("row", "col")
-    arrived = lax.all_to_all(
-        sending.reshape(supernodes, group_rows, column_total).astype(BF16), axes, split_axis=0, concat_axis=0, tiled=True
-    ).astype(F32)
-    arrived_pos = lax.all_to_all(places.reshape(supernodes, group_rows), axes, split_axis=0, concat_axis=0, tiled=True)
-    ordered = (
-        jnp.zeros_like(rhs_rows).at[arrived_pos.reshape(local_rows)].set(arrived.reshape(local_rows, column_total))
-    )
-    ordered = ordered.reshape(NLEV, B, column_total)
-    mask = block_mask.reshape(3, 128)
-    return solve(ordered, diag_inverse[:, 0], mask, lower_blocks)[:, None]
+    dest = dest_row.reshape(1, dest_row.shape[0])
+    return solve(rhs_rows, dest, diag_inverse[:, 0], block_mask, lower_blocks)[:, None]
 
 
 def solution(mesh):

time: 162 us -> 135 us (0.83)
  Pallas kernels: 112 us -> 133 us
  starting transfers between devices: 16.3 us -> 0 us
  waiting for transfers between devices: 14.3 us -> 0 us
  local copies, waits for them, and re-layouts: 12.6 us -> 1.67 us
  other arithmetic: 6.82 us -> 0 us
    pallas_call x1, Pallas kernels: 112 us -> 133 us  [solve(): pl.pallas_call(solve_kernel, out_shape=jax.ShapeDtypeStruct((NLEV, B, N),...]
    all_to_all x2 -> x0, starting transfers between devices: 16.3 us -> none  [the longest x1 11.5 us: per_device(): lax.all_to_all(places.reshape(supernodes, group_rows), axes, split_axis=0...]
    all_to_all x2 -> x0, waiting for transfers between devices: 14.3 us -> none  [the longest x1 7.26 us: per_device(): lax.all_to_all(sending.reshape(supernodes, group_rows, column_total).asty...]
    gather x2 -> x0, local copies, waits for them, and re-layouts: 5.05 us -> none  [the longest x1 3.49 us: per_device(): places = position[sort_order]]
    sort x1 -> x0, other arithmetic: 3.77 us -> none  [per_device(): sort_order = jnp.argsort(owner_idx, stable=True)]
    scatter x1 -> x0, local copies, waits for them, and re-layouts: 3.02 us -> none  [per_device(): jnp.zeros_like(rhs_rows).at[arrived_pos.reshape(local_rows)]]
  transfers between devices with their start and end apart: 2 -> 0, of which waited for: 2 -> 0; matrix products, arithmetic and copies ran while one was open for 4% -> 0% of each run, Pallas kernels for 0% -> 0%
where the time goes in v2:
time: 135 us; the launch traced here: 134 us
  Pallas kernels  133 us (99%)
  local copies, waits for them, and re-layouts  1.67 us (1%)
    pallas_call x1, Pallas kernels, solve(): pl.pallas_call(solve_kernel, out_shape=jax.ShapeDtypeStruct((NLEV, B, N),...  133 us

profile of v2, /device:TPU:1, one launch (start us, length us, event | category | flops | bytes accessed | tf_op | source)
XLA Modules:
  0.0 134.4 jit_solution(16789786008485924814)
XLA Ops:
  0.0 132.7 %shard_map.55 = bf16[4,128,256]{2,1,0:T(8,128)(2,1)} custom-call(f32[512,256]{1,0:T(8,128)} %rhs_ref.1, s32[1,512]{1,0:T(1,128)} %bitcast.7, bf16[4,128,128]{2,1,0:T(8,128)(2,1)} %bitcast.6, s32[3,1,8,1,16]{4,3,2,1,0:T(1,128)} %mask_ref.1, bf16[3,1,8,128,1,16,128]{6,5,4,3,2,1,0:T(8,128)(2,1)} %w_hbm.1), custom_call_target="tpu_custom_call" | custom-call | tf_op jit(solution)/shard_map/pallas_call | solution.py:358
  132.7 1.7 %copy.8 = bf16[4,1,128,256]{3,2,1,0:T(8,128)(2,1)} copy(bf16[4,1,128,256]{3,2,1,0:T(8,128)(2,1)} %bitcast.5) | data formatting | bytes 524288

commit v3 on v2

--- a/solution.py
+++ b/solution.py
@@ -30,9 +30,9 @@
 
 
 def solve_kernel(
-    rhs_ref, dest_ref, diag_ref, mask_ref, w_hbm, out_ref,
-    rows_out, rows_in, meta_out, meta_in, meta_sib, mix_out, mix_in, ordered_ref, raw, wd, gath, acc, sib_out, sib_in, z_out, z_in, solved_t, upper, part_out, part_in, line_out, line_in,
-    rows_s, rows_r, meta_s, meta_r, mix_s, mix_r, load_sem, ag_s, ag_r, sib_s, sib_r, z_s, z_r, up_s, up_r, fw_s, fw_r, p1_s, p1_r, p2_s, p2_r,
+    rhs_ref, dest_ref, diag_ref, mask_ref, w_hbm, out_hbm,
+    hello, out_ref,     rows_out, rows_in, meta_out, meta_in, meta_sib, mix_out, mix_in, ordered_ref, raw, wd, gath, acc, sib_out, sib_in, z_out, z_in, solved_t, upper, part_out, part_in, line_out, line_in,
+    rows_s, rows_r, meta_s, meta_r, mix_s, mix_r, load_sem, out_sem, ag_s, ag_r, sib_s, sib_r, z_s, z_r, up_s, up_r, fw_s, fw_r, p1_s, p1_r, p2_s, p2_r,
 ):
     row = lax.axis_index("row")
     col = lax.axis_index("col")
@@ -62,14 +62,16 @@
         t = (chip + k) % 64
         return t, (t // 4, (t % 4) * 2 + core)
 
+    def line(axis):
+        if axis == "x":
+            return [(row_of(0, x + d, y), col) for d in (1, 2, 3)]
+        return [(row_of(0, x, y + d), col) for d in (1, 2, 3)]
+
+    near = [(row_of(0, x + a, y), ((z + b) % 4) * 2 + core) for a in range(4) for b in range(4) if a or b]
+    near += line("y") + [sibling]
     barrier = pltpu.get_barrier_semaphore()
-    pl.semaphore_signal(barrier, inc=1, device_id=sibling, device_id_type=MESH)
-
-    def greet(k, carry):
-        pl.semaphore_signal(barrier, inc=1, device_id=chip_peer(k)[1], device_id_type=MESH)
-        return carry
-
-    lax.fori_loop(1, 64, greet, 0)
+    for dev in near:
+        pl.semaphore_signal(barrier, inc=1, device_id=dev, device_id_type=MESH)
 
     loads = [pltpu.make_async_copy(w_hbm.at[l, 0, :, :, 0], raw.at[l], load_sem.at[l]) for l in range(3)]
     for load in loads:
@@ -102,6 +104,11 @@
         solved = dot(diag_ref[l], residual).astype(BF16)
         return solved
 
+    def prepare(l, carry):
+        loads_wait(l)
+        relayout(l)
+        return carry
+
     dest = dest_ref[...]
     owner = (dest >> 7) & 127
     place = (dest >> 14) * B + (dest & 127)
@@ -122,7 +129,11 @@
     def meta_copy(t, dev):
         return remote(meta_out.at[t], meta_in.at[chip], meta_s, meta_r, dev)
 
-    pl.semaphore_wait(barrier, 64)
+    pl.semaphore_wait(barrier, len(near))
+    for dev in line("y"):
+        pl.semaphore_signal(hello, inc=1, device_id=dev, device_id_type=MESH)
+    prepare(0, 0)
+    pl.semaphore_wait(hello, 3)
 
     def send_rows(k, carry):
         t, dev = chip_peer(k)
@@ -134,12 +145,7 @@
     rows_in[chip] = rows_out[chip]
     meta_in[chip] = meta_out[chip]
 
-    def prepare(l, carry):
-        loads_wait(l)
-        relayout(l)
-        return carry
-
-    lax.fori_loop(0, 3, prepare, 0)
+    lax.fori_loop(1, 3, prepare, 0)
 
     some = pl.ds(0, 63)
     all_rows = remote(rows_out.at[some], rows_in.at[some], rows_s, rows_r, sibling)
@@ -180,28 +186,31 @@
         return jnp.concatenate([gath[l, 0, p], gath[l, 1, p]], axis=1)
 
     def down(l, carry):
-        for h in range(2):
+        def send(h, e, d, relay):
             u, v = first if h == 0 else second
-            for d in (2, 1, 3):
-                gather_copy(l, h, row, d - 1, (row_of(h, u + d, v), col)).start()
-        for e in (0, 1, 3, 2):
+            slot = row_of(h, u - e, v) if relay else row
+            target = row_of(h, u if relay else u + e, v + d)
+            gather_copy(l, h, slot, e - 1 if d == 0 else 3 + e * 3 + d - 1, (target, col)).start()
+
+        for e, d in ((1, 0), (3, 0), (0, 2), (0, 1), (0, 3), (2, 0), (2, 2), (2, 1), (2, 3)):
+            for h in range(2):
+                send(h, e, d, False)
+        for e in (1, 3):
             for h in range(2):
                 u, v = first if h == 0 else second
-                slot = row_of(h, u - e, v)
-                if e:
-                    gather_copy(l, h, slot, e - 1, (row, col)).wait_recv()
+                gather_copy(l, h, row_of(h, u - e, v), e - 1, (row, col)).wait_recv()
                 for d in (2, 1, 3):
-                    gather_copy(l, h, slot, 3 + e * 3 + d - 1, (row_of(h, u, v + d), col)).start()
-        order = [(a, b) for a in (0, 1, 3) for b in (0, 1, 3)] + [(a, b) for a in range(4) for b in range(4) if 2 in (a, b)]
-        done = set()
+                    send(h, e, d, True)
+        order = [(0, 0), (0, 1), (0, 3), (1, 0), (3, 0), (0, 2), (2, 0), (2, 2), (1, 1), (1, 3), (3, 1), (3, 3), (1, 2), (2, 1), (2, 3), (3, 2)]
+        batches = [order[:8], order[8:12], order[12:]]
 
         def arrive(a, b):
             for h in range(2):
                 e, d = (a, b) if h == 0 else (b, a)
                 u, v = first if h == 0 else second
-                if d and (h, e, d) not in done:
-                    done.add((h, e, d))
-                    gather_copy(l, h, row_of(h, u - e, v - d), 3 + e * 3 + d - 1, (row, col)).wait_recv()
+                if d or e == 2:
+                    index = 3 + e * 3 + d - 1 if d else e - 1
+                    gather_copy(l, h, row_of(h, u - e, v - d), index, (row, col)).wait_recv()
 
         def operands(some):
             slots = [row_of(0, x - a, y - b) for a, b in some]
@@ -211,15 +220,16 @@
         def lhs(slots, c, r, n):
             return jnp.concatenate([wd[l, p, c, r:r + n].reshape(n * B, B) for p in slots], axis=1)
 
-        for a, b in order[:8]:
-            arrive(a, b)
-        slots, rhs = operands(order[:8])
-        for c in range(2):
-            for r in range(0, 4, 2):
-                acc[c, r:r + 2] = dot(lhs(slots, c, r, 2), rhs).reshape(2, B, N)
-        for a, b in order[8:]:
-            arrive(a, b)
-        slots, rhs = operands(order[8:])
+        for index, batch in enumerate(batches):
+            for a, b in batch:
+                arrive(a, b)
+            slots, rhs = operands(batch)
+            if index == 2:
+                break
+            for c in range(2):
+                for r in range(0, 4, 2):
+                    part = dot(lhs(slots, c, r, 2), rhs).reshape(2, B, N)
+                    acc[c, r:r + 2] = part if index == 0 else acc[c, r:r + 2] + part
         for step, c in enumerate((other, core)):
             for half in range(2):
                 r = ((z // 2 + 1 - half) % 2) * 2
@@ -257,8 +267,15 @@
         upper[slot, core, z] = sol_t
         return sol_t
 
+    def out_copy(l):
+        return pltpu.make_async_copy(out_ref.at[l], out_hbm.at[l], out_sem.at[l])
+
+    def emit(l, sol_t):
+        out_ref[l] = sol_t.astype(F32).T.astype(BF16)
+        out_copy(l).start()
+
     top = finish(3, 0, solved_t[3])
-    out_ref[3] = top.astype(F32).T.astype(BF16)
+    emit(3, top)
 
     def up_copy(t, d):
         return remote(upper.at[t, core, z], upper.at[t, core, z], up_s.at[t, d - 1], up_r.at[t, d - 1], z_peer(d))
@@ -271,7 +288,7 @@
         u, v = first if h == 0 else second
         return remote(
             part_out.at[t, h, du, dv], part_in.at[t, h, du, dv],
-            p1_s.at[t, h, du, dv], p1_r.at[t, h, du, dv], (row_of(h, u + du, v), col),
+            p1_s.at[t, h, du, dv], p1_r.at[t, h, du, dv], (row_of(h, u + du, v + dv if du == 2 else v), col),
         )
 
     def line_copy(t, h, dv):
@@ -293,9 +310,10 @@
             slot = upper.at[t, other, (z - d) % 4]
             remote(slot, slot, fw_s.at[t, d], fw_r.at[t, d], sibling).wait_recv()
         left = jnp.concatenate([upper[t, c, r] for c in range(2) for r in range(4)], axis=1)
-        pairs = [((2, 2), (2, 1)), ((2, 3), (2, 0)), ((1, 2), (3, 2)), ((0, 2), (1, 1)),
-                 ((1, 3), (3, 1)), ((3, 3), (1, 0)), ((3, 0), (0, 1)), ((0, 3), (0, 0))]
-        for two in pairs:
+        pairs = [((1, 1), (1, 3)), ((3, 1), (3, 3)), ((1, 2), (3, 2)), ((2, 1), (2, 3)),
+                 ((2, 2), (0, 2)), ((2, 0), (0, 1)), ((1, 0), (0, 3)), ((3, 0), (0, 0))]
+        later = []
+        for index, two in enumerate(pairs):
             slots = [row_of(0, x + a, y + b) for a, b in two]
             right = jnp.concatenate([wd[l, p].reshape(8 * B, B) for p in slots], axis=1)
             value = dot(left, right).astype(BF16)
@@ -303,49 +321,68 @@
                 for h in range(2):
                     du, dv = (a, b) if h == 0 else (b, a)
                     part_out[t, h, du, dv] = value[h * B:(h + 1) * B, s * B:(s + 1) * B]
-                    if du:
+                    if du == 2 and index < 4:
+                        later.append((h, du, dv))
+                    elif du:
                         part_copy(t, h, du, dv).start()
+            if index == 3:
+                for h, du, dv in later:
+                    part_copy(t, h, du, dv).start()
+
+        def piece(h, du, dv):
+            part_copy(t, h, du, dv).wait_recv()
+            return part_in[t, h, du, dv].astype(F32)
+
+        for dv in (2, 1, 3):
+            for h in range(2):
+                total = part_out[t, h, 0, dv].astype(F32) + piece(h, 1, dv) + piece(h, 3, dv)
+                line_out[t, h, dv] = total.astype(BF16)
+                line_copy(t, h, dv).start()
         keep = []
-        for dv in (2, 1, 3, 0):
-            for h in range(2):
-                total = part_out[t, h, 0, dv].astype(F32)
-                for du in (1, 3, 2):
-                    part_copy(t, h, du, dv).wait_recv()
-                    total = total + part_in[t, h, du, dv].astype(F32)
-                if dv:
-                    line_out[t, h, dv] = total.astype(BF16)
-                    line_copy(t, h, dv).start()
-                else:
-                    keep.append(total)
+        for h in range(2):
+            total = part_out[t, h, 0, 0].astype(F32)
+            for du, dv in ((1, 0), (3, 0), (2, 0), (2, 1), (2, 3), (2, 2)):
+                total = total + piece(h, du, dv)
+            keep.append(total)
         for h in range(2):
             for dv in (1, 3, 2):
                 line_copy(t, h, dv).wait_recv()
                 keep[h] = keep[h] + line_in[t, h, dv].astype(F32)
         residual_t = solved_t[l] - jnp.concatenate(keep, axis=0)
         sol_t = finish(l, t + 1, residual_t)
-        out_ref[l] = sol_t.astype(F32).T.astype(BF16)
+        emit(l, sol_t)
         return carry
 
     lax.fori_loop(0, 3, up, 0)
 
-    def drain(l, carry):
+    def drain_down(l, carry):
         for h in range(2):
             for idx in range(15):
                 gather_copy(l, h, row, idx, (row, col)).wait_send()
+        for s in range(4):
+            remote(sib_out.at[l, s], sib_in.at[l, s], sib_s.at[l, s], sib_r.at[l, s], sibling).wait_send()
+        for d in range(1, 4):
+            remote(z_out.at[l, d - 1], z_in.at[l, d - 1], z_s.at[l, d - 1], z_r.at[l, d - 1], z_peer(d)).wait_send()
+        return carry
+
+    lax.fori_loop(0, 3, drain_down, 0)
+
+    def drain_up(t, carry):
+        for h in range(2):
             for du in range(1, 4):
                 for dv in range(4):
-                    part_copy(l, h, du, dv).wait_send()
+                    part_copy(t, h, du, dv).wait_send()
             for dv in range(1, 4):
-                line_copy(l, h, dv).wait_send()
-        for s in range(4):
-            remote(sib_out.at[l, s], sib_in.at[l, s], sib_s.at[l, s], sib_r.at[l, s], sibling).wait_send()
-            forward_copy(l, s).wait_send()
-        for d in range(1, 4):
-            remote(z_out.at[l, d - 1], z_in.at[l, d - 1], z_s.at[l, d - 1], z_r.at[l, d - 1], z_peer(d)).wait_send()
-            up_copy(l, d).wait_send()
-        return carry
-
-    lax.fori_loop(0, 3, drain, 0)
+                line_copy(t, h, dv).wait_send()
+        for d in range(4):
+            forward_copy(t, d).wait_send()
+            if d:
+                up_copy(t, d).wait_send()
+        return carry
+
+    lax.fori_loop(0, 3, drain_up, 0)
+    for l in range(NLEV):
+        out_copy(l).wait()
     all_rows.wait_send()
     all_meta.wait_send()
     meta_swap.wait_send()
@@ -359,8 +396,10 @@
         solve_kernel,
         out_shape=jax.ShapeDtypeStruct((NLEV, B, N), BF16),
         in_specs=[vmem, vmem, vmem, pl.BlockSpec(memory_space=pltpu.SMEM), pl.BlockSpec(memory_space=pl.ANY)],
-        out_specs=vmem,
+        out_specs=pl.BlockSpec(memory_space=pl.ANY),
         scratch_shapes=[
+            pltpu.SemaphoreType.REGULAR,
+            pltpu.VMEM((NLEV, B, N), BF16),
             pltpu.VMEM((64, 8, N), BF16),
             pltpu.VMEM((64, 8, N), BF16),
             pltpu.VMEM((64, 1, B), F32),
@@ -384,12 +423,12 @@
             pltpu.VMEM((3, 2, 4, B, B), BF16),
             pltpu.VMEM((3, 2, 4, B, B), BF16),
             dma, dma, dma, dma, dma((2,)), dma((2,)),
-            dma((3,)), dma((3, 2, 15)), dma((3, 2, 15)), dma((3, 4)), dma((3, 4)), dma((3, 3)), dma((3, 3)),
+            dma((3,)), dma((NLEV,)), dma((3, 2, 15)), dma((3, 2, 15)), dma((3, 4)), dma((3, 4)), dma((3, 3)), dma((3, 3)),
             dma((3, 3)), dma((3, 3)), dma((3, 4)), dma((3, 4)),
             dma((3, 2, 4, 4)), dma((3, 2, 4, 4)), dma((3, 2, 4)), dma((3, 2, 4)),
         ],
         compiler_params=pltpu.CompilerParams(
-            collective_id=0, has_side_effects=True, vmem_limit_bytes=60 * 1024 * 1024
+            collective_id=0, has_side_effects=True, vmem_limit_bytes=50 * 1024 * 1024
         ),
     )(rhs, dest, diag, mask, lower)
 

time: 135 us -> 144 us (1.067)
  Pallas kernels: 133 us -> 140 us
  local copies, waits for them, and re-layouts: 1.67 us -> 4.04 us
    pallas_call x1, Pallas kernels: 133 us -> 140 us  [solve(): pl.pallas_call(solve_kernel, out_shape=jax.ShapeDtypeStruct((NLEV, B, N),...]
    unnamed x1 -> x9, local copies, waits for them, and re-layouts: 1.67 us -> 4.04 us
where the time goes in v3:
time: 144 us
  Pallas kernels  140 us (97%)
  local copies, waits for them, and re-layouts  4.04 us (3%)
    pallas_call x1, Pallas kernels, solve(): pl.pallas_call(solve_kernel, out_shape=jax.ShapeDtypeStruct((NLEV, B, N),...  140 us
    unnamed x9, local copies, waits for them, and re-layouts  4.04 us

profile of v3, /device:TPU:1, one launch (start us, length us, event | category | flops | bytes accessed | tf_op | source)
XLA Modules:
  0.0 144.0 jit_solution(11781781396125527243)
XLA Ops:
  0.0 0.0 copy-start
  0.0 1.0 copy-done
  1.0 0.0 copy-start.1
  1.0 0.9 copy-done.1
  1.9 0.0 copy-start.2
  1.9 0.7 copy-done.2
  2.7 0.0 copy-start.3
  2.7 0.7 copy-done.3
  3.3 140.0 %shard_map.55 = bf16[4,128,256]{2,1,0:T(8,128)(2,1)S(1)} custom-call(f32[512,256]{1,0:T(8,128)S(1)} %copy-done, s32[1,512]{1,0:T(1,128)S(1)} %bitcast.7, bf16[4,128,128]{2,1,0:T(8,128)(2,1)S(1)} %bitcast.6, s32[3,1,8,1,16]{4,3,2,1,0:T(1,128)S(1)} %copy-done.2, bf16[3,1,8,128,1,16,128]{6,5,4,3,2,1,0:T(8,128)(2,1)} %w_hbm.1), custom_call_target="tpu_custom_call" | custom-call | tf_op jit(solution)/shard_map/pallas_call | solution.py:395
  143.3 0.7 copy.8
Async XLA Ops:
  0.0 1.0 copy-start
  1.0 0.9 copy-start.1
  1.9 0.7 copy-start.2
  2.7 0.7 copy-start.3

commit v4 on v3

--- a/solution.py
+++ b/solution.py
@@ -30,9 +30,9 @@
 
 
 def solve_kernel(
-    rhs_ref, dest_ref, diag_ref, mask_ref, w_hbm, out_hbm,
-    hello, out_ref,     rows_out, rows_in, meta_out, meta_in, meta_sib, mix_out, mix_in, ordered_ref, raw, wd, gath, acc, sib_out, sib_in, z_out, z_in, solved_t, upper, part_out, part_in, line_out, line_in,
-    rows_s, rows_r, meta_s, meta_r, mix_s, mix_r, load_sem, out_sem, ag_s, ag_r, sib_s, sib_r, z_s, z_r, up_s, up_r, fw_s, fw_r, p1_s, p1_r, p2_s, p2_r,
+    rhs_hbm, dest_hbm, diag_hbm, mask_hbm, w_hbm, out_hbm,
+    hello, rhs_ref, dest_ref, diag_ref, mask_ref, out_ref,     rows_out, rows_in, meta_out, meta_in, meta_sib, mix_out, mix_in, ordered_ref, raw, wd, gath, acc, sib_out, sib_in, z_out, z_in, solved_t, upper, part_out, part_in, line_out, line_in,
+    rows_s, rows_r, meta_s, meta_r, mix_s, mix_r, in_sem, load_sem, out_sem, ag_s, ag_r, sib_s, sib_r, z_s, z_r, up_s, up_r, fw_s, fw_r, p1_s, p1_r, p2_s, p2_r,
 ):
     row = lax.axis_index("row")
     col = lax.axis_index("col")
@@ -67,6 +67,10 @@
             return [(row_of(0, x + d, y), col) for d in (1, 2, 3)]
         return [(row_of(0, x, y + d), col) for d in (1, 2, 3)]
 
+    inputs = [(dest_hbm, dest_ref), (rhs_hbm, rhs_ref), (mask_hbm, mask_ref), (diag_hbm, diag_ref)]
+    inputs = [pltpu.make_async_copy(src, dst, in_sem.at[i]) for i, (src, dst) in enumerate(inputs)]
+    for copy in inputs:
+        copy.start()
     near = [(row_of(0, x + a, y), ((z + b) % 4) * 2 + core) for a in range(4) for b in range(4) if a or b]
     near += line("y") + [sibling]
     barrier = pltpu.get_barrier_semaphore()
@@ -109,6 +113,8 @@
         relayout(l)
         return carry
 
+    for copy in inputs[:2]:
+        copy.wait()
     dest = dest_ref[...]
     owner = (dest >> 7) & 127
     place = (dest >> 14) * B + (dest & 127)
@@ -132,6 +138,8 @@
     pl.semaphore_wait(barrier, len(near))
     for dev in line("y"):
         pl.semaphore_signal(hello, inc=1, device_id=dev, device_id_type=MESH)
+    for copy in inputs[2:]:
+        copy.wait()
     prepare(0, 0)
     pl.semaphore_wait(hello, 3)
 
@@ -186,31 +194,26 @@
         return jnp.concatenate([gath[l, 0, p], gath[l, 1, p]], axis=1)
 
     def down(l, carry):
-        def send(h, e, d, relay):
+        for h in range(2):
             u, v = first if h == 0 else second
-            slot = row_of(h, u - e, v) if relay else row
-            target = row_of(h, u if relay else u + e, v + d)
-            gather_copy(l, h, slot, e - 1 if d == 0 else 3 + e * 3 + d - 1, (target, col)).start()
-
-        for e, d in ((1, 0), (3, 0), (0, 2), (0, 1), (0, 3), (2, 0), (2, 2), (2, 1), (2, 3)):
-            for h in range(2):
-                send(h, e, d, False)
-        for e in (1, 3):
+            for d in (2, 1, 3):
+                gather_copy(l, h, row, d - 1, (row_of(h, u + d, v), col)).start()
+        for e in (0, 1, 3, 2):
             for h in range(2):
                 u, v = first if h == 0 else second
-                gather_copy(l, h, row_of(h, u - e, v), e - 1, (row, col)).wait_recv()
+                slot = row_of(h, u - e, v)
+                if e:
+                    gather_copy(l, h, slot, e - 1, (row, col)).wait_recv()
                 for d in (2, 1, 3):
-                    send(h, e, d, True)
-        order = [(0, 0), (0, 1), (0, 3), (1, 0), (3, 0), (0, 2), (2, 0), (2, 2), (1, 1), (1, 3), (3, 1), (3, 3), (1, 2), (2, 1), (2, 3), (3, 2)]
-        batches = [order[:8], order[8:12], order[12:]]
+                    gather_copy(l, h, slot, 3 + e * 3 + d - 1, (row_of(h, u, v + d), col)).start()
+        order = [(a, b) for a in (0, 1, 3) for b in (0, 1, 3)] + [(a, b) for a in range(4) for b in range(4) if 2 in (a, b)]
 
         def arrive(a, b):
             for h in range(2):
                 e, d = (a, b) if h == 0 else (b, a)
                 u, v = first if h == 0 else second
-                if d or e == 2:
-                    index = 3 + e * 3 + d - 1 if d else e - 1
-                    gather_copy(l, h, row_of(h, u - e, v - d), index, (row, col)).wait_recv()
+                if d:
+                    gather_copy(l, h, row_of(h, u - e, v - d), 3 + e * 3 + d - 1, (row, col)).wait_recv()
 
         def operands(some):
             slots = [row_of(0, x - a, y - b) for a, b in some]
@@ -220,16 +223,15 @@
         def lhs(slots, c, r, n):
             return jnp.concatenate([wd[l, p, c, r:r + n].reshape(n * B, B) for p in slots], axis=1)
 
-        for index, batch in enumerate(batches):
-            for a, b in batch:
-                arrive(a, b)
-            slots, rhs = operands(batch)
-            if index == 2:
-                break
-            for c in range(2):
-                for r in range(0, 4, 2):
-                    part = dot(lhs(slots, c, r, 2), rhs).reshape(2, B, N)
-                    acc[c, r:r + 2] = part if index == 0 else acc[c, r:r + 2] + part
+        for a, b in order[:8]:
+            arrive(a, b)
+        slots, rhs = operands(order[:8])
+        for c in range(2):
+            for r in range(0, 4, 2):
+                acc[c, r:r + 2] = dot(lhs(slots, c, r, 2), rhs).reshape(2, B, N)
+        for a, b in order[8:]:
+            arrive(a, b)
+        slots, rhs = operands(order[8:])
         for step, c in enumerate((other, core)):
             for half in range(2):
                 r = ((z // 2 + 1 - half) % 2) * 2
@@ -288,7 +290,7 @@
         u, v = first if h == 0 else second
         return remote(
             part_out.at[t, h, du, dv], part_in.at[t, h, du, dv],
-            p1_s.at[t, h, du, dv], p1_r.at[t, h, du, dv], (row_of(h, u + du, v + dv if du == 2 else v), col),
+            p1_s.at[t, h, du, dv], p1_r.at[t, h, du, dv], (row_of(h, u + du, v), col),
         )
 
     def line_copy(t, h, dv):
@@ -310,10 +312,9 @@
             slot = upper.at[t, other, (z - d) % 4]
             remote(slot, slot, fw_s.at[t, d], fw_r.at[t, d], sibling).wait_recv()
         left = jnp.concatenate([upper[t, c, r] for c in range(2) for r in range(4)], axis=1)
-        pairs = [((1, 1), (1, 3)), ((3, 1), (3, 3)), ((1, 2), (3, 2)), ((2, 1), (2, 3)),
-                 ((2, 2), (0, 2)), ((2, 0), (0, 1)), ((1, 0), (0, 3)), ((3, 0), (0, 0))]
-        later = []
-        for index, two in enumerate(pairs):
+        pairs = [((2, 2), (2, 1)), ((2, 3), (1, 2)), ((3, 2), (1, 1)), ((1, 3), (3, 1)),
+                 ((3, 3), (0, 2)), ((2, 0), (0, 1)), ((1, 0), (0, 3)), ((3, 0), (0, 0))]
+        for two in pairs:
             slots = [row_of(0, x + a, y + b) for a, b in two]
             right = jnp.concatenate([wd[l, p].reshape(8 * B, B) for p in slots], axis=1)
             value = dot(left, right).astype(BF16)
@@ -321,29 +322,23 @@
                 for h in range(2):
                     du, dv = (a, b) if h == 0 else (b, a)
                     part_out[t, h, du, dv] = value[h * B:(h + 1) * B, s * B:(s + 1) * B]
-                    if du == 2 and index < 4:
-                        later.append((h, du, dv))
-                    elif du:
+                    if du:
                         part_copy(t, h, du, dv).start()
-            if index == 3:
-                for h, du, dv in later:
-                    part_copy(t, h, du, dv).start()
-
-        def piece(h, du, dv):
-            part_copy(t, h, du, dv).wait_recv()
-            return part_in[t, h, du, dv].astype(F32)
+
+        def line_sum(h, dv):
+            total = part_out[t, h, 0, dv].astype(F32)
+            for du in (1, 3, 2):
+                part_copy(t, h, du, dv).wait_recv()
+                total = total + part_in[t, h, du, dv].astype(F32)
+            return total
 
         for dv in (2, 1, 3):
             for h in range(2):
-                total = part_out[t, h, 0, dv].astype(F32) + piece(h, 1, dv) + piece(h, 3, dv)
-                line_out[t, h, dv] = total.astype(BF16)
+                line_out[t, h, dv] = line_sum(h, dv).astype(BF16)
                 line_copy(t, h, dv).start()
         keep = []
         for h in range(2):
-            total = part_out[t, h, 0, 0].astype(F32)
-            for du, dv in ((1, 0), (3, 0), (2, 0), (2, 1), (2, 3), (2, 2)):
-                total = total + piece(h, du, dv)
-            keep.append(total)
+            keep.append(line_sum(h, 0))
         for h in range(2):
             for dv in (1, 3, 2):
                 line_copy(t, h, dv).wait_recv()
@@ -390,15 +385,19 @@
 
 
 def solve(rhs, dest, diag, mask, lower):
-    vmem = pl.BlockSpec(memory_space=pltpu.VMEM)
+    hbm = pl.BlockSpec(memory_space=pltpu.HBM)
     dma = pltpu.SemaphoreType.DMA
     return pl.pallas_call(
         solve_kernel,
         out_shape=jax.ShapeDtypeStruct((NLEV, B, N), BF16),
-        in_specs=[vmem, vmem, vmem, pl.BlockSpec(memory_space=pltpu.SMEM), pl.BlockSpec(memory_space=pl.ANY)],
+        in_specs=[hbm] * 5,
         out_specs=pl.BlockSpec(memory_space=pl.ANY),
         scratch_shapes=[
             pltpu.SemaphoreType.REGULAR,
+            pltpu.VMEM(rhs.shape, F32),
+            pltpu.VMEM(dest.shape, jnp.int32),
+            pltpu.VMEM(diag.shape, BF16),
+            pltpu.SMEM(mask.shape, jnp.int32),
             pltpu.VMEM((NLEV, B, N), BF16),
             pltpu.VMEM((64, 8, N), BF16),
             pltpu.VMEM((64, 8, N), BF16),
@@ -423,14 +422,14 @@
             pltpu.VMEM((3, 2, 4, B, B), BF16),
             pltpu.VMEM((3, 2, 4, B, B), BF16),
             dma, dma, dma, dma, dma((2,)), dma((2,)),
-            dma((3,)), dma((NLEV,)), dma((3, 2, 15)), dma((3, 2, 15)), dma((3, 4)), dma((3, 4)), dma((3, 3)), dma((3, 3)),
+            dma((4,)), dma((3,)), dma((NLEV,)), dma((3, 2, 15)), dma((3, 2, 15)), dma((3, 4)), dma((3, 4)), dma((3, 3)), dma((3, 3)),
             dma((3, 3)), dma((3, 3)), dma((3, 4)), dma((3, 4)),
             dma((3, 2, 4, 4)), dma((3, 2, 4, 4)), dma((3, 2, 4)), dma((3, 2, 4)),
         ],
         compiler_params=pltpu.CompilerParams(
             collective_id=0, has_side_effects=True, vmem_limit_bytes=50 * 1024 * 1024
         ),
-    )(rhs, dest, diag, mask, lower)
+    )(*[pltpu.with_memory_space_constraint(a, pltpu.HBM) for a in (rhs, dest, diag, mask, lower)])
 
 
 def per_device(rhs_rows, dest_row, diag_inverse, lower_blocks, block_mask):

time: 144 us -> 131 us (0.910)
  Pallas kernels: 140 us -> 130 us
  local copies, waits for them, and re-layouts: 4.04 us -> 0.71 us
    pallas_call x1, Pallas kernels: 140 us -> 130 us  [solve(): pl.pallas_call(solve_kernel, out_shape=jax.ShapeDtypeStruct((NLEV, B, N),...]
    unnamed x9 -> x1, local copies, waits for them, and re-layouts: 4.04 us -> 0.71 us
where the time goes in v4:
time: 131 us
  Pallas kernels  130 us (99%)
    pallas_call x1, Pallas kernels, solve(): pl.pallas_call(solve_kernel, out_shape=jax.ShapeDtypeStruct((NLEV, B, N),...  130 us

profile of v4, /device:TPU:1, one launch (start us, length us, event | category | flops | bytes accessed | tf_op | source)
XLA Modules:
  0.0 130.6 jit_solution(561576462654369003)
XLA Ops:
  0.0 129.9 %shard_map.55 = bf16[4,128,256]{2,1,0:T(8,128)(2,1)S(1)} custom-call(f32[512,256]{1,0:T(8,128)} %rhs_hbm.1, s32[1,512]{1,0:T(1,128)} %bitcast.7, bf16[4,128,128]{2,1,0:T(8,128)(2,1)} %bitcast.6, s32[3,1,8,1,16]{4,3,2,1,0:T(1,128)} %mask_hbm.1, bf16[3,1,8,128,1,16,128]{6,5,4,3,2,1,0:T(8,128)(2,1)} %w_hbm.1), custom_call_target="tpu_custom_call" | custom-call | tf_op jit(solution)/shard_map/pallas_call | solution.py:390
  129.9 0.7 copy.8

commit v5 on v4

v5 whole, which is shorter than its diff:
```python
import jax
import jax.numpy as jnp
from jax import lax
from jax.experimental import pallas as pl
from jax.experimental.pallas import tpu as pltpu
from jax.sharding import PartitionSpec as P

B = 128
NLEV = 4
N = 256
C = 128
H = 64
MESH = pl.DeviceIdType.MESH
F32 = jnp.float32
BF16 = jnp.bfloat16


def dot(a, b):
    return jnp.dot(a, b, preferred_element_type=F32)


def dot_rows(a, b):
    return lax.dot_general(a, b, (((1,), (1,)), ((), ())), preferred_element_type=F32)


def one_hot(condition):
    return jnp.where(condition, 1.0, 0.0).astype(BF16)


def iota(shape, axis):
    return lax.broadcasted_iota(jnp.int32, shape, axis)


def solve_kernel(
    rhs_hbm, dest_hbm, diag_hbm, mask_hbm, w_hbm, out_hbm,
    hello, rhs_ref, dest_ref, diag_ref, mask_ref, out_ref,     rows_out, rows_in, meta_out, meta_in, meta_sib, mix_out, mix_in, ordered_ref, raw, wd, gath, acc, sib_out, sib_in, z_out, z_in, solved_t, upper, part_out, part_in, line_out, line_in,
    rows_s, rows_r, meta_s, meta_r, mix_s, mix_r, in_sem, load_sem, out_sem, ag_s, ag_r, sib_s, sib_r, z_s, z_r, up_s, up_r, fw_s, fw_r, p1_s, p1_r, p2_s, p2_r,
):
    row = lax.axis_index("row")
    col = lax.axis_index("col")
    x, y = row // 4, row % 4
    z, core = col // 2, col % 2
    other = 1 - core

    def row_of(h, u, v):
        return (u % 4) * 4 + v % 4 if h == 0 else (v % 4) * 4 + u % 4

    def remote(src, dst, ssem, rsem, dev):
        return pltpu.make_async_remote_copy(
            src_ref=src, dst_ref=dst, send_sem=ssem, recv_sem=rsem, device_id=dev, device_id_type=MESH
        )

    sibling = (row, z * 2 + other)

    def z_peer(d):
        return (row, ((z + d) % 4) * 2 + core)

    chip = row * 4 + z

    def chip_peer(k):
        t = (chip + k) % 64
        return t, (t // 4, (t % 4) * 2 + core)

    def line(axis):
        if axis == "x":
            return [(row_of(0, x + d, y), col) for d in (1, 2, 3)]
        return [(row_of(0, x, y + d), col) for d in (1, 2, 3)]

    inputs = [(dest_hbm, dest_ref), (rhs_hbm, rhs_ref), (mask_hbm, mask_ref), (diag_hbm, diag_ref)]
    inputs = [pltpu.make_async_copy(src, dst, in_sem.at[i]) for i, (src, dst) in enumerate(inputs)]
    for copy in inputs:
        copy.start()
    near = [(row_of(0, x + a, y), ((z + b) % 4) * 2 + core) for a in range(4) for b in range(4) if a or b]
    near += line("y") + [sibling]
    barrier = pltpu.get_barrier_semaphore()
    for dev in near:
        pl.semaphore_signal(barrier, inc=1, device_id=dev, device_id_type=MESH)

    loads = [pltpu.make_async_copy(w_hbm.at[l, 0, :, :, 0], raw.at[l], load_sem.at[l]) for l in range(3)]
    for load in loads:
        load.start()

    def loads_wait(l):
        pltpu.make_async_copy(w_hbm.at[l, 0, :, :, 0], raw.at[l], load_sem.at[l]).wait()

    out_row, in_row = iota((256, 256), 0), iota((256, 256), 1)
    perm = one_hot(in_row == (out_row & 15) * 16 + (out_row >> 4))

    def relayout(l):
        def one(i, carry):
            zz, cc = i // 2, i % 2
            scale = [mask_ref[l, 0, i, 0, p].astype(F32) for p in range(16)]
            for k0 in range(0, 8, 2):
                piece = jnp.concatenate(
                    [raw[l, i, (k0 + s) * 16:(k0 + s + 1) * 16].reshape(256, B) for s in range(2)], axis=1
                )
                moved = dot(perm, piece)
                for p in range(16):
                    for s in range(2):
                        tile = moved[p * 16:(p + 1) * 16, s * B:(s + 1) * B] * scale[p]
                        wd[l, p, cc, zz, (k0 + s) * 16:(k0 + s + 1) * 16, :] = tile.astype(BF16)
            return carry

        lax.fori_loop(0, 8, one, 0)

    def prepare(l, carry):
        loads_wait(l)
        relayout(l)
        return carry

    for copy in inputs[:2]:
        copy.wait()
    dest = dest_ref[...]
    owner = (dest >> 7) & 127
    place = (dest >> 14) * B + (dest & 127)
    owned = one_hot(iota((128, 512), 0) == owner)
    before = dot(owned, one_hot(iota((512, 512), 0) < iota((512, 512), 1)))
    rank = jnp.sum(owned.astype(F32) * before, axis=0, keepdims=True)
    slot = owner * 4 + rank.astype(jnp.int32)
    sort = one_hot(iota((512, 512), 0) == slot)
    rows_out[...] = dot(sort, rhs_ref[...].astype(BF16)).astype(BF16).reshape(64, 8, N)
    lane = iota((128, 512), 0)
    digit = jnp.where(lane < 8, place >> 4, place & 15)
    digit = jnp.where((lane < 16) & ((lane & 7) == (slot & 7)), digit, 0).astype(F32).astype(BF16)
    meta_out[...] = dot_rows(one_hot(iota((64, 512), 0) == (slot >> 3)), digit).reshape(64, 1, B)

    def rows_copy(t, dev):
        return remote(rows_out.at[t], rows_in.at[chip], rows_s, rows_r, dev)

    def meta_copy(t, dev):
        return remote(meta_out.at[t], meta_in.at[chip], meta_s, meta_r, dev)

    pl.semaphore_wait(barrier, len(near))
    for dev in line("y"):
        pl.semaphore_signal(hello, inc=1, device_id=dev, device_id_type=MESH)
    for copy in inputs[2:]:
        copy.wait()
    prepare(0, 0)
    pl.semaphore_wait(hello, 3)

    def send_rows(k, carry):
        t, dev = chip_peer(k)
        meta_copy(t, dev).start()
        rows_copy(t, dev).start()
        return carry

    lax.fori_loop(1, 64, send_rows, 0)
    rows_in[chip] = rows_out[chip]
    meta_in[chip] = meta_out[chip]

    lax.fori_loop(1, 3, prepare, 0)

    some = pl.ds(0, 63)
    all_rows = remote(rows_out.at[some], rows_in.at[some], rows_s, rows_r, sibling)
    all_meta = remote(meta_out.at[some], meta_in.at[some], meta_s, meta_r, sibling)
    all_meta.wait_recv()
    meta_swap = remote(meta_in, meta_sib, mix_s.at[0], mix_r.at[0], sibling)
    meta_swap.start()
    all_rows.wait_recv()
    to, at = iota((512, 512), 0), iota((512, 512), 1)
    half = jnp.where(to < 256, core, other)
    mixed = dot(one_hot(at == (to & 63) * 8 + half * 4 + ((to >> 6) & 3)), rows_in[...].reshape(512, N)).astype(BF16)
    mix_out[...] = mixed[256:]
    mix_swap = remote(mix_out, mix_in, mix_s.at[1], mix_r.at[1], sibling)
    mix_swap.start()

    def place_rows(meta, rows):
        digits = jnp.concatenate([meta.reshape(64, B)] * 4, axis=0)
        at_lane, k = iota((256, B), 1), iota((256, B), 0) >> 6
        mine = (at_lane < 16) & ((at_lane & 7) == core * 4 + k)
        weight = jnp.where(iota((8, B), 1) < 8, 16.0, 1.0).astype(BF16)
        where = dot_rows(weight, jnp.where(mine, digits, 0.0).astype(BF16))[:1]
        return dot(one_hot(iota((512, 256), 0) == where.astype(jnp.int32)), rows)

    total = place_rows(meta_in[...], mixed[:256])
    meta_swap.wait_recv()
    mix_swap.wait_recv()
    ordered_ref[...] = (total + place_rows(meta_sib[...], mix_in[...])).reshape(NLEV, B, N)

    def set_solved(l, s, residual):
        solved = dot(diag_ref[l], residual).astype(BF16)
        gath[l, s, row] = solved
        solved_t[l, s] = solved.astype(F32).T

    def axes(h):
        return (x, y) if h == 0 else (y, x)

    def gather_copy(l, s, h, slot, idx, dev):
        rows = gath.at[l, s, slot, pl.ds(h * H, H)]
        return remote(rows, rows, ag_s.at[l, s, h, idx], ag_r.at[l, s, h, idx], dev)

    def relay(l, s, h, e):
        u, v = axes(h)
        slot = row_of(h, u - e, v)
        if e:
            gather_copy(l, s, h, slot, e - 1, (row, col)).wait_recv()
        for d in (2, 1, 3):
            gather_copy(l, s, h, slot, 3 + e * 3 + d - 1, (row_of(h, u, v + d), col)).start()

    def down_send(l, s):
        for h in range(2):
            u, v = axes(h)
            for d in (2, 1, 3):
                gather_copy(l, s, h, row, d - 1, (row_of(h, u + d, v), col)).start()
        for h in range(2):
            relay(l, s, h, 0)

    def down_relay(l, s):
        for e in (1, 3, 2):
            for h in range(2):
                relay(l, s, h, e)

    order = [(a, b) for a in (0, 1, 3) for b in (0, 1, 3)] + [(a, b) for a in range(4) for b in range(4) if 2 in (a, b)]

    def operands(l, s, some):
        slots = [row_of(0, x - a, y - b) for a, b in some]
        for a, b in some:
            for h in range(2):
                e, d = (a, b) if h == 0 else (b, a)
                u, v = axes(h)
                if d:
                    gather_copy(l, s, h, row_of(h, u - e, v - d), 3 + e * 3 + d - 1, (row, col)).wait_recv()
        return slots, jnp.concatenate([gath[l, s, p] for p in slots], axis=0)

    def down_first(l, s):
        slots, rhs = operands(l, s, order[:8])
        for c in range(2):
            for r in range(0, 4, 2):
                left = jnp.concatenate([wd[l, p, c, r:r + 2].reshape(2 * B, B) for p in slots], axis=1)
                acc[s, c, r:r + 2] = dot(left, rhs).reshape(2, B, C)

    def sib_copy(l, s, zz, send):
        return remote(sib_out.at[l, s, zz], sib_in.at[l, s, zz], sib_s.at[l, s, send], sib_r.at[l, s, zz], sibling)

    def z_copy(l, s, d):
        return remote(z_out.at[l, s, d - 1], z_in.at[l, s, d - 1], z_s.at[l, s, d - 1], z_r.at[l, s, d - 1], z_peer(d))

    def down_second(l, s):
        slots, rhs = operands(l, s, order[8:])
        for step, c in enumerate((other, core)):
            for half in range(2):
                r = ((z // 2 + 1 - half) % 2) * 2
                left = jnp.concatenate([wd[l, p, c, pl.ds(r, 2)].reshape(2 * B, B) for p in slots], axis=1)
                total = acc[s, c, pl.ds(r, 2)] + dot(left, rhs).reshape(2, B, C)
                if step == 0:
                    sib_out[l, s, pl.ds(r, 2)] = total.astype(BF16)
                    for k in range(2):
                        sib_copy(l, s, r + k, half * 2 + k).start()
                else:
                    acc[s, c, pl.ds(r, 2)] = total

    def chip_sum(l, s, d):
        zz = (z + d) % 4
        sib_copy(l, s, zz, 0).wait_recv()
        return acc[s, core, zz] + sib_in[l, s, zz].astype(F32)

    def down_line(l, s):
        for d in (2, 1, 3):
            z_out[l, s, d - 1] = chip_sum(l, s, d).astype(BF16)
            z_copy(l, s, d).start()

    def down_finish(l, s):
        own = ordered_ref[l + 1, :, s * C:(s + 1) * C] - chip_sum(l, s, 0)
        for d in (1, 3, 2):
            z_copy(l, s, d).wait_recv()
            own = own - z_in[l, s, d - 1].astype(F32)
        set_solved(l + 1, s, own.astype(BF16))

    def out_copy(l):
        return pltpu.make_async_copy(out_ref.at[l], out_hbm.at[l], out_sem.at[l])

    def finish(l, slot, s, residual_t):
        sol_t = dot(residual_t.astype(BF16), diag_ref[l]).astype(BF16)
        upper[slot, s, core, z] = sol_t
        return sol_t

    def emit(l, s, sol_t):
        out_ref[l, :, s * C:(s + 1) * C] = sol_t.astype(F32).T.astype(BF16)
        if s == 1:
            out_copy(l).start()

    def up_copy(t, s, d):
        slot = upper.at[t, s, core, z]
        return remote(slot, slot, up_s.at[t, s, d - 1], up_r.at[t, s, d - 1], z_peer(d))

    def forward_copy(t, s, d):
        slot = upper.at[t, s, core, (z - d) % 4]
        return remote(slot, slot, fw_s.at[t, s, d], fw_r.at[t, s, d], sibling)

    def part_copy(t, s, h, du, dv):
        u, v = axes(h)
        return remote(
            part_out.at[t, s, h, du, dv], part_in.at[t, s, h, du, dv],
            p1_s.at[t, s, h, du, dv], p1_r.at[t, s, h, du, dv], (row_of(h, u + du, v), col),
        )

    def line_copy(t, s, h, dv):
        u, v = axes(h)
        return remote(
            line_out.at[t, s, h, dv], line_in.at[t, s, h, dv],
            p2_s.at[t, s, h, dv], p2_r.at[t, s, h, dv], (row_of(h, u, v + dv), col),
        )

    def up_send(t, s):
        for d in (2, 1, 3):
            up_copy(t, s, d).start()
        forward_copy(t, s, 0).start()

    def up_forward(t, s):
        for d in (1, 3, 2):
            slot = upper.at[t, s, core, (z - d) % 4]
            remote(slot, slot, up_s.at[t, s, d - 1], up_r.at[t, s, d - 1], sibling).wait_recv()
            forward_copy(t, s, d).start()

    def up_parts(t, s):
        for d in (0, 1, 3, 2):
            slot = upper.at[t, s, other, (z - d) % 4]
            remote(slot, slot, fw_s.at[t, s, d], fw_r.at[t, s, d], sibling).wait_recv()
        left = jnp.concatenate([upper[t, s, c, r] for c in range(2) for r in range(4)], axis=1)
        pairs = [((2, 2), (2, 1)), ((2, 3), (1, 2)), ((3, 2), (1, 1)), ((1, 3), (3, 1)),
                 ((3, 3), (0, 2)), ((2, 0), (0, 1)), ((1, 0), (0, 3)), ((3, 0), (0, 0))]
        for two in pairs:
            slots = [row_of(0, x + a, y + b) for a, b in two]
            right = jnp.concatenate([wd[2 - t, p].reshape(8 * B, B) for p in slots], axis=1)
            value = dot(left, right).astype(BF16)
            for k, (a, b) in enumerate(two):
                for h in range(2):
                    du, dv = (a, b) if h == 0 else (b, a)
                    part_out[t, s, h, du, dv] = value[h * H:(h + 1) * H, k * B:(k + 1) * B]
                    if du:
                        part_copy(t, s, h, du, dv).start()

    def line_sum(t, s, h, dv):
        total = part_out[t, s, h, 0, dv].astype(F32)
        for du in (1, 3, 2):
            part_copy(t, s, h, du, dv).wait_recv()
            total = total + part_in[t, s, h, du, dv].astype(F32)
        return total

    def up_lines(t, s):
        for dv in (2, 1, 3):
            for h in range(2):
                line_out[t, s, h, dv] = line_sum(t, s, h, dv).astype(BF16)
                line_copy(t, s, h, dv).start()

    def up_finish(t, s):
        keep = []
        for h in range(2):
            total = line_sum(t, s, h, 0)
            for dv in (1, 3, 2):
                line_copy(t, s, h, dv).wait_recv()
                total = total + line_in[t, s, h, dv].astype(F32)
            keep.append(total)
        residual_t = solved_t[2 - t, s] - jnp.concatenate(keep, axis=0)
        emit(2 - t, s, finish(2 - t, t + 1, s, residual_t))

    def top(s):
        emit(3, s, finish(3, 0, s, solved_t[3, s]))

    for s in range(2):
        set_solved(0, s, ordered_ref[0, :, s * C:(s + 1) * C].astype(BF16))

    def down(l, carry):
        down_send(l, 0)

        @pl.when(l > 0)
        def _():
            down_first(l - 1, 1)
            down_second(l - 1, 1)
            down_line(l - 1, 1)

        down_relay(l, 0)

        @pl.when(l > 0)
        def _():
            down_finish(l - 1, 1)

        down_send(l, 1)
        down_first(l, 0)
        down_second(l, 0)
        down_line(l, 0)
        down_relay(l, 1)
        down_finish(l, 0)
        return carry

    lax.fori_loop(0, 3, down, 0)
    top(0)

    def up(t, carry):
        up_send(t, 0)

        @pl.when(t == 0)
        def _():
            down_first(2, 1)
            down_second(2, 1)
            down_line(2, 1)

        @pl.when(t > 0)
        def _():
            up_lines(t - 1, 1)

        up_forward(t, 0)
        up_parts(t, 0)

        @pl.when(t == 0)
        def _():
            down_finish(2, 1)
            top(1)

        @pl.when(t > 0)
        def _():
            up_finish(t - 1, 1)

        up_send(t, 1)
        up_lines(t, 0)
        up_forward(t, 1)
        up_parts(t, 1)
        up_finish(t, 0)
        return carry

    lax.fori_loop(0, 3, up, 0)
    up_lines(2, 1)
    up_finish(2, 1)

    def drain_down(l, carry):
        for s in range(2):
            for h in range(2):
                for idx in range(15):
                    gather_copy(l, s, h, row, idx, (row, col)).wait_send()
            for k in range(4):
                sib_copy(l, s, k, k).wait_send()
            for d in range(1, 4):
                z_copy(l, s, d).wait_send()
        return carry

    lax.fori_loop(0, 3, drain_down, 0)

    def drain_up(t, carry):
        for s in range(2):
            for h in range(2):
                for du in range(1, 4):
                    for dv in range(4):
                        part_copy(t, s, h, du, dv).wait_send()
                for dv in range(1, 4):
                    line_copy(t, s, h, dv).wait_send()
            for d in range(4):
                forward_copy(t, s, d).wait_send()
                if d:
                    up_copy(t, s, d).wait_send()
        return carry

    lax.fori_loop(0, 3, drain_up, 0)
    for l in range(NLEV):
        out_copy(l).wait()
    all_rows.wait_send()
    all_meta.wait_send()
    meta_swap.wait_send()
    mix_swap.wait_send()


def solve(rhs, dest, diag, mask, lower):
    hbm = pl.BlockSpec(memory_space=pltpu.HBM)
    dma = pltpu.SemaphoreType.DMA
    return pl.pallas_call(
        solve_kernel,
        out_shape=jax.ShapeDtypeStruct((NLEV, B, N), BF16),
        in_specs=[hbm] * 5,
        out_specs=pl.BlockSpec(memory_space=pl.ANY),
        scratch_shapes=[
            pltpu.SemaphoreType.REGULAR,
            pltpu.VMEM(rhs.shape, F32),
            pltpu.VMEM(dest.shape, jnp.int32),
            pltpu.VMEM(diag.shape, BF16),
            pltpu.SMEM(mask.shape, jnp.int32),
            pltpu.VMEM((NLEV, B, N), BF16),
            pltpu.VMEM((64, 8, N), BF16),
            pltpu.VMEM((64, 8, N), BF16),
            pltpu.VMEM((64, 1, B), F32),
            pltpu.VMEM((64, 1, B), F32),
            pltpu.VMEM((64, 1, B), F32),
            pltpu.VMEM((256, N), BF16),
            pltpu.VMEM((256, N), BF16),
            pltpu.VMEM((NLEV, B, N), F32),
            pltpu.VMEM((3, 8, B, 16, B), BF16),
            pltpu.VMEM((3, 16, 2, 4, B, B), BF16),
            pltpu.VMEM((4, 2, 16, B, C), BF16),
            pltpu.VMEM((2, 2, 4, B, C), F32),
            pltpu.VMEM((3, 2, 4, B, C), BF16),
            pltpu.VMEM((3, 2, 4, B, C), BF16),
            pltpu.VMEM((3, 2, 3, B, C), BF16),
            pltpu.VMEM((3, 2, 3, B, C), BF16),
            pltpu.VMEM((4, 2, C, B), F32),
            pltpu.VMEM((4, 2, 2, 4, C, B), BF16),
            pltpu.VMEM((3, 2, 2, 4, 4, H, B), BF16),
            pltpu.VMEM((3, 2, 2, 4, 4, H, B), BF16),
            pltpu.VMEM((3, 2, 2, 4, H, B), BF16),
            pltpu.VMEM((3, 2, 2, 4, H, B), BF16),
            dma, dma, dma, dma, dma((2,)), dma((2,)),
            dma((4,)), dma((3,)), dma((NLEV,)), dma((3, 2, 2, 15)), dma((3, 2, 2, 15)), dma((3, 2, 4)), dma((3, 2, 4)),
            dma((3, 2, 3)), dma((3, 2, 3)), dma((3, 2, 3)), dma((3, 2, 3)), dma((3, 2, 4)), dma((3, 2, 4)),
            dma((3, 2, 2, 4, 4)), dma((3, 2, 2, 4, 4)), dma((3, 2, 2, 4)), dma((3, 2, 2, 4)),
        ],
        compiler_params=pltpu.CompilerParams(
            collective_id=0, has_side_effects=True, vmem_limit_bytes=50 * 1024 * 1024
        ),
    )(*[pltpu.with_memory_space_constraint(a, pltpu.HBM) for a in (rhs, dest, diag, mask, lower)])


def per_device(rhs_rows, dest_row, diag_inverse, lower_blocks, block_mask):
    dest = dest_row.reshape(1, dest_row.shape[0])
    return solve(rhs_rows, dest, diag_inverse[:, 0], block_mask, lower_blocks)[:, None]


def solution(mesh):
    in_specs = (
        P(("row", "col"), None),
        P(("row", "col")),
        P(None, ("row", "col"), None, None),
        P(None, "row", None, None, "col", None, None),
        P(None, "row", None, "col", None),
    )
    out_specs = P(None, ("row", "col"), None, None)
    return jax.shard_map(per_device, mesh=mesh, in_specs=in_specs, out_specs=out_specs, check_vma=False)
```

time: 131 us -> 123 us (0.939)
  Pallas kernels: 130 us -> 123 us
    pallas_call x1, Pallas kernels: 130 us -> 123 us  [solve(): pl.pallas_call(solve_kernel, out_shape=jax.ShapeDtypeStruct((NLEV, B, N),...]
where the time goes in v5:
time: 123 us
  Pallas kernels  123 us (100%)
    pallas_call x1, Pallas kernels, solve(): pl.pallas_call(solve_kernel, out_shape=jax.ShapeDtypeStruct((NLEV, B, N),...  123 us

profile of v5, /device:TPU:1, one launch (start us, length us, event | category | flops | bytes accessed | tf_op | source)
XLA Modules:
  0.0 123.4 jit_solution(7757895408142231181)
XLA Ops:
  0.0 122.7 %shard_map.55 = bf16[4,128,256]{2,1,0:T(8,128)(2,1)S(1)} custom-call(f32[512,256]{1,0:T(8,128)} %rhs_hbm.1, s32[1,512]{1,0:T(1,128)} %bitcast.7, bf16[4,128,128]{2,1,0:T(8,128)(2,1)} %bitcast.6, s32[3,1,8,1,16]{4,3,2,1,0:T(1,128)} %mask_hbm.1, bf16[3,1,8,128,1,16,128]{6,5,4,3,2,1,0:T(8,128)(2,1)} %w_hbm.1), custom_call_target="tpu_custom_call" | custom-call | tf_op jit(solution)/shard_map/pallas_call | solution.py:464
  122.7 0.7 copy.8

commit v6 on v5

--- a/solution.py
+++ b/solution.py
@@ -33,8 +33,8 @@
 
 def solve_kernel(
     rhs_hbm, dest_hbm, diag_hbm, mask_hbm, w_hbm, out_hbm,
-    hello, rhs_ref, dest_ref, diag_ref, mask_ref, out_ref,     rows_out, rows_in, meta_out, meta_in, meta_sib, mix_out, mix_in, ordered_ref, raw, wd, gath, acc, sib_out, sib_in, z_out, z_in, solved_t, upper, part_out, part_in, line_out, line_in,
-    rows_s, rows_r, meta_s, meta_r, mix_s, mix_r, in_sem, load_sem, out_sem, ag_s, ag_r, sib_s, sib_r, z_s, z_r, up_s, up_r, fw_s, fw_r, p1_s, p1_r, p2_s, p2_r,
+    hello, rhs_ref, dest_ref, diag_ref, mask_ref, out_ref,     rows_out, rows_in, meta_out, meta_in, meta_sib, mix_out, mix_in, ordered_ref, raw, wd, gath, acc, col_out, col_in, solved_t, upper, part_out, part_in, line_out, line_in,
+    rows_s, rows_r, meta_s, meta_r, mix_s, mix_r, in_sem, load_sem, out_sem, ag_s, ag_r, col_s, col_r, up_s, up_r, fw_s, fw_r, p1_s, p1_r, p2_s, p2_r,
 ):
     row = lax.axis_index("row")
     col = lax.axis_index("col")
@@ -187,7 +187,7 @@
 
     def gather_copy(l, s, h, slot, idx, dev):
         rows = gath.at[l, s, slot, pl.ds(h * H, H)]
-        return remote(rows, rows, ag_s.at[l, s, h, idx], ag_r.at[l, s, h, idx], dev)
+        return remote(rows, rows, ag_s.at[l, s], ag_r.at[l, s, h, idx], dev)
 
     def relay(l, s, h, e):
         u, v = axes(h)
@@ -229,41 +229,32 @@
                 left = jnp.concatenate([wd[l, p, c, r:r + 2].reshape(2 * B, B) for p in slots], axis=1)
                 acc[s, c, r:r + 2] = dot(left, rhs).reshape(2, B, C)
 
-    def sib_copy(l, s, zz, send):
-        return remote(sib_out.at[l, s, zz], sib_in.at[l, s, zz], sib_s.at[l, s, send], sib_r.at[l, s, zz], sibling)
-
-    def z_copy(l, s, d):
-        return remote(z_out.at[l, s, d - 1], z_in.at[l, s, d - 1], z_s.at[l, s, d - 1], z_r.at[l, s, d - 1], z_peer(d))
+    def col_copy(l, s, dc, zz):
+        d = (zz - z + 4) % 4
+        return remote(
+            col_out.at[l, s, dc, zz], col_in.at[l, s, dc, d], col_s.at[l, s], col_r.at[l, s, dc, d],
+            (row, zz * 2 + (other if dc else core)),
+        )
 
     def down_second(l, s):
         slots, rhs = operands(l, s, order[8:])
-        for step, c in enumerate((other, core)):
-            for half in range(2):
-                r = ((z // 2 + 1 - half) % 2) * 2
+        for half in range(2):
+            r = ((z // 2 + 1 - half) % 2) * 2
+            for dc, c in ((1, other), (0, core)):
                 left = jnp.concatenate([wd[l, p, c, pl.ds(r, 2)].reshape(2 * B, B) for p in slots], axis=1)
                 total = acc[s, c, pl.ds(r, 2)] + dot(left, rhs).reshape(2, B, C)
-                if step == 0:
-                    sib_out[l, s, pl.ds(r, 2)] = total.astype(BF16)
-                    for k in range(2):
-                        sib_copy(l, s, r + k, half * 2 + k).start()
+                col_out[l, s, dc, pl.ds(r, 2)] = total.astype(BF16)
+                if half == 0 or dc == 1:
+                    col_copy(l, s, dc, r + z % 2).start()
                 else:
                     acc[s, c, pl.ds(r, 2)] = total
-
-    def chip_sum(l, s, d):
-        zz = (z + d) % 4
-        sib_copy(l, s, zz, 0).wait_recv()
-        return acc[s, core, zz] + sib_in[l, s, zz].astype(F32)
-
-    def down_line(l, s):
-        for d in (2, 1, 3):
-            z_out[l, s, d - 1] = chip_sum(l, s, d).astype(BF16)
-            z_copy(l, s, d).start()
+                col_copy(l, s, dc, r + 1 - z % 2).start()
 
     def down_finish(l, s):
-        own = ordered_ref[l + 1, :, s * C:(s + 1) * C] - chip_sum(l, s, 0)
-        for d in (1, 3, 2):
-            z_copy(l, s, d).wait_recv()
-            own = own - z_in[l, s, d - 1].astype(F32)
+        own = ordered_ref[l + 1, :, s * C:(s + 1) * C] - acc[s, core, z]
+        for dc, d in ((1, 0), (0, 1), (0, 3), (0, 2), (1, 1), (1, 3), (1, 2)):
+            remote(col_out.at[l, s, dc, 0], col_in.at[l, s, dc, d], col_s.at[l, s], col_r.at[l, s, dc, d], sibling).wait_recv()
+            own = own - col_in[l, s, dc, d].astype(F32)
         set_solved(l + 1, s, own.astype(BF16))
 
     def out_copy(l):
@@ -281,24 +272,24 @@
 
     def up_copy(t, s, d):
         slot = upper.at[t, s, core, z]
-        return remote(slot, slot, up_s.at[t, s, d - 1], up_r.at[t, s, d - 1], z_peer(d))
+        return remote(slot, slot, up_s.at[t, s], up_r.at[t, s, d - 1], z_peer(d))
 
     def forward_copy(t, s, d):
         slot = upper.at[t, s, core, (z - d) % 4]
-        return remote(slot, slot, fw_s.at[t, s, d], fw_r.at[t, s, d], sibling)
+        return remote(slot, slot, fw_s.at[t, s], fw_r.at[t, s, d], sibling)
 
     def part_copy(t, s, h, du, dv):
         u, v = axes(h)
         return remote(
             part_out.at[t, s, h, du, dv], part_in.at[t, s, h, du, dv],
-            p1_s.at[t, s, h, du, dv], p1_r.at[t, s, h, du, dv], (row_of(h, u + du, v), col),
+            p1_s.at[t, s], p1_r.at[t, s, h, du, dv], (row_of(h, u + du, v), col),
         )
 
     def line_copy(t, s, h, dv):
         u, v = axes(h)
         return remote(
             line_out.at[t, s, h, dv], line_in.at[t, s, h, dv],
-            p2_s.at[t, s, h, dv], p2_r.at[t, s, h, dv], (row_of(h, u, v + dv), col),
+            p2_s.at[t, s], p2_r.at[t, s, h, dv], (row_of(h, u, v + dv), col),
         )
 
     def up_send(t, s):
@@ -309,13 +300,13 @@
     def up_forward(t, s):
         for d in (1, 3, 2):
             slot = upper.at[t, s, core, (z - d) % 4]
-            remote(slot, slot, up_s.at[t, s, d - 1], up_r.at[t, s, d - 1], sibling).wait_recv()
+            remote(slot, slot, up_s.at[t, s], up_r.at[t, s, d - 1], sibling).wait_recv()
             forward_copy(t, s, d).start()
 
     def up_parts(t, s):
         for d in (0, 1, 3, 2):
             slot = upper.at[t, s, other, (z - d) % 4]
-            remote(slot, slot, fw_s.at[t, s, d], fw_r.at[t, s, d], sibling).wait_recv()
+            remote(slot, slot, fw_s.at[t, s], fw_r.at[t, s, d], sibling).wait_recv()
         left = jnp.concatenate([upper[t, s, c, r] for c in range(2) for r in range(4)], axis=1)
         pairs = [((2, 2), (2, 1)), ((2, 3), (1, 2)), ((3, 2), (1, 1)), ((1, 3), (3, 1)),
                  ((3, 3), (0, 2)), ((2, 0), (0, 1)), ((1, 0), (0, 3)), ((3, 0), (0, 0))]
@@ -367,7 +358,6 @@
         def _():
             down_first(l - 1, 1)
             down_second(l - 1, 1)
-            down_line(l - 1, 1)
 
         down_relay(l, 0)
 
@@ -378,7 +368,6 @@
         down_send(l, 1)
         down_first(l, 0)
         down_second(l, 0)
-        down_line(l, 0)
         down_relay(l, 1)
         down_finish(l, 0)
         return carry
@@ -393,7 +382,6 @@
         def _():
             down_first(2, 1)
             down_second(2, 1)
-            down_line(2, 1)
 
         @pl.when(t > 0)
         def _():
@@ -422,34 +410,23 @@
     up_lines(2, 1)
     up_finish(2, 1)
 
-    def drain_down(l, carry):
+    def drain(l, carry):
         for s in range(2):
-            for h in range(2):
-                for idx in range(15):
-                    gather_copy(l, s, h, row, idx, (row, col)).wait_send()
-            for k in range(4):
-                sib_copy(l, s, k, k).wait_send()
-            for d in range(1, 4):
-                z_copy(l, s, d).wait_send()
+            blocks = gath.at[l, s, pl.ds(0, 15)]
+            remote(blocks, blocks, ag_s.at[l, s], ag_r.at[l, s, 0, 0], sibling).wait_send()
+            blocks = gath.at[l, s, pl.ds(0, 7)]
+            remote(blocks, blocks, col_s.at[l, s], col_r.at[l, s, 0, 0], sibling).wait_send()
+            blocks = part_out.at[l, s, :, pl.ds(0, 3)]
+            remote(blocks, blocks, p1_s.at[l, s], p1_r.at[l, s, 0, 0, 0], sibling).wait_send()
+            blocks = line_out.at[l, s, :, pl.ds(0, 3)]
+            remote(blocks, blocks, p2_s.at[l, s], p2_r.at[l, s, 0, 0], sibling).wait_send()
+            blocks = upper.at[l, s, 0, pl.ds(0, 3)]
+            remote(blocks, blocks, up_s.at[l, s], up_r.at[l, s, 0], sibling).wait_send()
+            blocks = upper.at[l, s, 0]
+            remote(blocks, blocks, fw_s.at[l, s], fw_r.at[l, s, 0], sibling).wait_send()
         return carry
 
-    lax.fori_loop(0, 3, drain_down, 0)
-
-    def drain_up(t, carry):
-        for s in range(2):
-            for h in range(2):
-                for du in range(1, 4):
-                    for dv in range(4):
-                        part_copy(t, s, h, du, dv).wait_send()
-                for dv in range(1, 4):
-                    line_copy(t, s, h, dv).wait_send()
-            for d in range(4):
-                forward_copy(t, s, d).wait_send()
-                if d:
-                    up_copy(t, s, d).wait_send()
-        return carry
-
-    lax.fori_loop(0, 3, drain_up, 0)
+    lax.fori_loop(0, 3, drain, 0)
     for l in range(NLEV):
         out_copy(l).wait()
     all_rows.wait_send()
@@ -485,10 +462,8 @@
             pltpu.VMEM((3, 16, 2, 4, B, B), BF16),
             pltpu.VMEM((4, 2, 16, B, C), BF16),
             pltpu.VMEM((2, 2, 4, B, C), F32),
-            pltpu.VMEM((3, 2, 4, B, C), BF16),
-            pltpu.VMEM((3, 2, 4, B, C), BF16),
-            pltpu.VMEM((3, 2, 3, B, C), BF16),
-            pltpu.VMEM((3, 2, 3, B, C), BF16),
+            pltpu.VMEM((3, 2, 2, 4, B, C), BF16),
+            pltpu.VMEM((3, 2, 2, 4, B, C), BF16),
             pltpu.VMEM((4, 2, C, B), F32),
             pltpu.VMEM((4, 2, 2, 4, C, B), BF16),
             pltpu.VMEM((3, 2, 2, 4, 4, H, B), BF16),
@@ -496,9 +471,9 @@
             pltpu.VMEM((3, 2, 2, 4, H, B), BF16),
             pltpu.VMEM((3, 2, 2, 4, H, B), BF16),
             dma, dma, dma, dma, dma((2,)), dma((2,)),
-            dma((4,)), dma((3,)), dma((NLEV,)), dma((3, 2, 2, 15)), dma((3, 2, 2, 15)), dma((3, 2, 4)), dma((3, 2, 4)),
-            dma((3, 2, 3)), dma((3, 2, 3)), dma((3, 2, 3)), dma((3, 2, 3)), dma((3, 2, 4)), dma((3, 2, 4)),
-            dma((3, 2, 2, 4, 4)), dma((3, 2, 2, 4, 4)), dma((3, 2, 2, 4)), dma((3, 2, 2, 4)),
+            dma((4,)), dma((3,)), dma((NLEV,)), dma((3, 2)), dma((3, 2, 2, 15)), dma((3, 2)), dma((3, 2, 2, 4)),
+            dma((3, 2)), dma((3, 2, 3)), dma((3, 2)), dma((3, 2, 4)),
+            dma((3, 2)), dma((3, 2, 2, 4, 4)), dma((3, 2)), dma((3, 2, 2, 4)),
         ],
         compiler_params=pltpu.CompilerParams(
             collective_id=0, has_side_effects=True, vmem_limit_bytes=50 * 1024 * 1024

time: 123 us -> 118 us (0.959)
  Pallas kernels: 123 us -> 117 us
    pallas_call x1, Pallas kernels: 123 us -> 117 us  [solve(): pl.pallas_call(solve_kernel, out_shape=jax.ShapeDtypeStruct((NLEV, B, N),...]
where the time goes in v6:
time: 118 us
  Pallas kernels  117 us (99%)
    pallas_call x1, Pallas kernels, solve(): pl.pallas_call(solve_kernel, out_shape=jax.ShapeDtypeStruct((NLEV, B, N),...  117 us

profile of v6, /device:TPU:1, one launch (start us, length us, event | category | flops | bytes accessed | tf_op | source)
XLA Modules:
  0.0 117.5 jit_solution(5381532791502980350)
XLA Ops:
  0.0 116.8 %shard_map.55 = bf16[4,128,256]{2,1,0:T(8,128)(2,1)S(1)} custom-call(f32[512,256]{1,0:T(8,128)} %rhs_hbm.1, s32[1,512]{1,0:T(1,128)} %bitcast.7, bf16[4,128,128]{2,1,0:T(8,128)(2,1)} %bitcast.6, s32[3,1,8,1,16]{4,3,2,1,0:T(1,128)} %mask_hbm.1, bf16[3,1,8,128,1,16,128]{6,5,4,3,2,1,0:T(8,128)(2,1)} %w_hbm.1), custom_call_target="tpu_custom_call" | custom-call | tf_op jit(solution)/shard_map/pallas_call | solution.py:441
  116.8 0.7 copy.8

commit v7 on v6

--- a/solution.py
+++ b/solution.py
@@ -33,7 +33,7 @@
 
 def solve_kernel(
     rhs_hbm, dest_hbm, diag_hbm, mask_hbm, w_hbm, out_hbm,
-    hello, rhs_ref, dest_ref, diag_ref, mask_ref, out_ref,     rows_out, rows_in, meta_out, meta_in, meta_sib, mix_out, mix_in, ordered_ref, raw, wd, gath, acc, col_out, col_in, solved_t, upper, part_out, part_in, line_out, line_in,
+    hello, rhs_ref, dest_ref, diag_ref, mask_ref, out_ref,     rows_out, rows_in, meta_out, meta_in, meta_sib, mix_out, mix_in, mixer, placer, ordered_ref, raw, wd, gath, acc, col_out, col_in, solved_t, upper, part_out, part_in, line_out, line_in,
     rows_s, rows_r, meta_s, meta_r, mix_s, mix_r, in_sem, load_sem, out_sem, ag_s, ag_r, col_s, col_r, up_s, up_r, fw_s, fw_r, p1_s, p1_r, p2_s, p2_r,
 ):
     row = lax.axis_index("row")
@@ -77,8 +77,6 @@
         pl.semaphore_signal(barrier, inc=1, device_id=dev, device_id_type=MESH)
 
     loads = [pltpu.make_async_copy(w_hbm.at[l, 0, :, :, 0], raw.at[l], load_sem.at[l]) for l in range(3)]
-    for load in loads:
-        load.start()
 
     def loads_wait(l):
         pltpu.make_async_copy(w_hbm.at[l, 0, :, :, 0], raw.at[l], load_sem.at[l]).wait()
@@ -110,6 +108,8 @@
 
     for copy in inputs[:2]:
         copy.wait()
+    for load in loads:
+        load.start()
     dest = dest_ref[...]
     owner = (dest >> 7) & 127
     place = (dest >> 14) * B + (dest & 127)
@@ -153,29 +153,32 @@
     some = pl.ds(0, 63)
     all_rows = remote(rows_out.at[some], rows_in.at[some], rows_s, rows_r, sibling)
     all_meta = remote(meta_out.at[some], meta_in.at[some], meta_s, meta_r, sibling)
-    all_meta.wait_recv()
-    meta_swap = remote(meta_in, meta_sib, mix_s.at[0], mix_r.at[0], sibling)
-    meta_swap.start()
-    all_rows.wait_recv()
     to, at = iota((512, 512), 0), iota((512, 512), 1)
     half = jnp.where(to < 256, core, other)
-    mixed = dot(one_hot(at == (to & 63) * 8 + half * 4 + ((to >> 6) & 3)), rows_in[...].reshape(512, N)).astype(BF16)
-    mix_out[...] = mixed[256:]
-    mix_swap = remote(mix_out, mix_in, mix_s.at[1], mix_r.at[1], sibling)
-    mix_swap.start()
-
-    def place_rows(meta, rows):
+    mixer[...] = one_hot(at == (to & 63) * 8 + half * 4 + ((to >> 6) & 3))
+
+    def places(meta):
         digits = jnp.concatenate([meta.reshape(64, B)] * 4, axis=0)
         at_lane, k = iota((256, B), 1), iota((256, B), 0) >> 6
         mine = (at_lane < 16) & ((at_lane & 7) == core * 4 + k)
         weight = jnp.where(iota((8, B), 1) < 8, 16.0, 1.0).astype(BF16)
         where = dot_rows(weight, jnp.where(mine, digits, 0.0).astype(BF16))[:1]
-        return dot(one_hot(iota((512, 256), 0) == where.astype(jnp.int32)), rows)
-
-    total = place_rows(meta_in[...], mixed[:256])
+        return one_hot(iota((512, 256), 0) == where.astype(jnp.int32))
+
+    all_meta.wait_recv()
+    meta_swap = remote(meta_in, meta_sib, mix_s.at[0], mix_r.at[0], sibling)
+    meta_swap.start()
+    placer[0] = places(meta_in[...])
     meta_swap.wait_recv()
+    placer[1] = places(meta_sib[...])
+    all_rows.wait_recv()
+    arrived = rows_in[...].reshape(512, N)
+    mix_out[...] = dot(mixer[256:], arrived).astype(BF16)
+    mix_swap = remote(mix_out, mix_in, mix_s.at[1], mix_r.at[1], sibling)
+    mix_swap.start()
+    total = dot(placer[0], dot(mixer[:256], arrived).astype(BF16))
     mix_swap.wait_recv()
-    ordered_ref[...] = (total + place_rows(meta_sib[...], mix_in[...])).reshape(NLEV, B, N)
+    ordered_ref[...] = (total + dot(placer[1], mix_in[...])).reshape(NLEV, B, N)
 
     def set_solved(l, s, residual):
         solved = dot(diag_ref[l], residual).astype(BF16)
@@ -185,23 +188,29 @@
     def axes(h):
         return (x, y) if h == 0 else (y, x)
 
-    def gather_copy(l, s, h, slot, idx, dev):
+    order = [(a, b) for a in (0, 1, 3) for b in (0, 1, 3)] + [(a, b) for a in range(4) for b in range(4) if 2 in (a, b)]
+
+    def batch_of(h, e, d):
+        return 6 if ((e, d) if h == 0 else (d, e)) in order[:8] else 7
+
+    def gather_copy(l, s, h, slot, e, d, dev):
+        sem = batch_of(h, e, d) if d else h * 3 + e - 1
         rows = gath.at[l, s, slot, pl.ds(h * H, H)]
-        return remote(rows, rows, ag_s.at[l, s], ag_r.at[l, s, h, idx], dev)
+        return remote(rows, rows, ag_s.at[l, s], ag_r.at[l, s, sem], dev)
 
     def relay(l, s, h, e):
         u, v = axes(h)
         slot = row_of(h, u - e, v)
         if e:
-            gather_copy(l, s, h, slot, e - 1, (row, col)).wait_recv()
+            gather_copy(l, s, h, slot, e, 0, (row, col)).wait_recv()
         for d in (2, 1, 3):
-            gather_copy(l, s, h, slot, 3 + e * 3 + d - 1, (row_of(h, u, v + d), col)).start()
+            gather_copy(l, s, h, slot, e, d, (row_of(h, u, v + d), col)).start()
 
     def down_send(l, s):
         for h in range(2):
             u, v = axes(h)
             for d in (2, 1, 3):
-                gather_copy(l, s, h, row, d - 1, (row_of(h, u + d, v), col)).start()
+                gather_copy(l, s, h, row, d, 0, (row_of(h, u + d, v), col)).start()
         for h in range(2):
             relay(l, s, h, 0)
 
@@ -210,20 +219,16 @@
             for h in range(2):
                 relay(l, s, h, e)
 
-    order = [(a, b) for a in (0, 1, 3) for b in (0, 1, 3)] + [(a, b) for a in range(4) for b in range(4) if 2 in (a, b)]
-
-    def operands(l, s, some):
+    def operands(l, s, batch):
+        some = order[8 * batch:8 * batch + 8]
+        halves = sum((a != 0) + (b != 0) for a, b in some)
+        blocks = gath.at[l, s, pl.ds(0, halves // 2)]
+        remote(blocks, blocks, ag_s.at[l, s], ag_r.at[l, s, 6 + batch], sibling).wait_recv()
         slots = [row_of(0, x - a, y - b) for a, b in some]
-        for a, b in some:
-            for h in range(2):
-                e, d = (a, b) if h == 0 else (b, a)
-                u, v = axes(h)
-                if d:
-                    gather_copy(l, s, h, row_of(h, u - e, v - d), 3 + e * 3 + d - 1, (row, col)).wait_recv()
         return slots, jnp.concatenate([gath[l, s, p] for p in slots], axis=0)
 
     def down_first(l, s):
-        slots, rhs = operands(l, s, order[:8])
+        slots, rhs = operands(l, s, 0)
         for c in range(2):
             for r in range(0, 4, 2):
                 left = jnp.concatenate([wd[l, p, c, r:r + 2].reshape(2 * B, B) for p in slots], axis=1)
@@ -232,12 +237,12 @@
     def col_copy(l, s, dc, zz):
         d = (zz - z + 4) % 4
         return remote(
-            col_out.at[l, s, dc, zz], col_in.at[l, s, dc, d], col_s.at[l, s], col_r.at[l, s, dc, d],
+            col_out.at[l, s, dc, zz], col_in.at[l, s, dc, d], col_s.at[l, s], col_r.at[l, s],
             (row, zz * 2 + (other if dc else core)),
         )
 
     def down_second(l, s):
-        slots, rhs = operands(l, s, order[8:])
+        slots, rhs = operands(l, s, 1)
         for half in range(2):
             r = ((z // 2 + 1 - half) % 2) * 2
             for dc, c in ((1, other), (0, core)):
@@ -252,9 +257,11 @@
 
     def down_finish(l, s):
         own = ordered_ref[l + 1, :, s * C:(s + 1) * C] - acc[s, core, z]
-        for dc, d in ((1, 0), (0, 1), (0, 3), (0, 2), (1, 1), (1, 3), (1, 2)):
-            remote(col_out.at[l, s, dc, 0], col_in.at[l, s, dc, d], col_s.at[l, s], col_r.at[l, s, dc, d], sibling).wait_recv()
-            own = own - col_in[l, s, dc, d].astype(F32)
+        blocks = gath.at[l, s, pl.ds(0, 7)]
+        remote(blocks, blocks, col_s.at[l, s], col_r.at[l, s], sibling).wait_recv()
+        for dc in range(2):
+            for d in range(1 - dc, 4):
+                own = own - col_in[l, s, dc, d].astype(F32)
         set_solved(l + 1, s, own.astype(BF16))
 
     def out_copy(l):
@@ -276,20 +283,20 @@
 
     def forward_copy(t, s, d):
         slot = upper.at[t, s, core, (z - d) % 4]
-        return remote(slot, slot, fw_s.at[t, s], fw_r.at[t, s, d], sibling)
+        return remote(slot, slot, fw_s.at[t, s], fw_r.at[t, s], sibling)
 
     def part_copy(t, s, h, du, dv):
         u, v = axes(h)
         return remote(
             part_out.at[t, s, h, du, dv], part_in.at[t, s, h, du, dv],
-            p1_s.at[t, s], p1_r.at[t, s, h, du, dv], (row_of(h, u + du, v), col),
+            p1_s.at[t, s], p1_r.at[t, s, dv], (row_of(h, u + du, v), col),
         )
 
     def line_copy(t, s, h, dv):
         u, v = axes(h)
         return remote(
             line_out.at[t, s, h, dv], line_in.at[t, s, h, dv],
-            p2_s.at[t, s], p2_r.at[t, s, h, dv], (row_of(h, u, v + dv), col),
+            p2_s.at[t, s], p2_r.at[t, s], (row_of(h, u, v + dv), col),
         )
 
     def up_send(t, s):
@@ -304,9 +311,8 @@
             forward_copy(t, s, d).start()
 
     def up_parts(t, s):
-        for d in (0, 1, 3, 2):
-            slot = upper.at[t, s, other, (z - d) % 4]
-            remote(slot, slot, fw_s.at[t, s], fw_r.at[t, s, d], sibling).wait_recv()
+        slot = upper.at[t, s, other]
+        remote(slot, slot, fw_s.at[t, s], fw_r.at[t, s], sibling).wait_recv()
         left = jnp.concatenate([upper[t, s, c, r] for c in range(2) for r in range(4)], axis=1)
         pairs = [((2, 2), (2, 1)), ((2, 3), (1, 2)), ((3, 2), (1, 1)), ((1, 3), (3, 1)),
                  ((3, 3), (0, 2)), ((2, 0), (0, 1)), ((1, 0), (0, 3)), ((3, 0), (0, 0))]
@@ -321,27 +327,30 @@
                     if du:
                         part_copy(t, s, h, du, dv).start()
 
-    def line_sum(t, s, h, dv):
-        total = part_out[t, s, h, 0, dv].astype(F32)
-        for du in (1, 3, 2):
-            part_copy(t, s, h, du, dv).wait_recv()
-            total = total + part_in[t, s, h, du, dv].astype(F32)
-        return total
+    def line_sums(t, s, dv):
+        blocks = part_in.at[t, s, :, pl.ds(0, 3), 0]
+        remote(blocks, blocks, p1_s.at[t, s], p1_r.at[t, s, dv], sibling).wait_recv()
+        sums = []
+        for h in range(2):
+            total = part_out[t, s, h, 0, dv].astype(F32)
+            for du in (1, 3, 2):
+                total = total + part_in[t, s, h, du, dv].astype(F32)
+            sums.append(total)
+        return sums
 
     def up_lines(t, s):
         for dv in (2, 1, 3):
-            for h in range(2):
-                line_out[t, s, h, dv] = line_sum(t, s, h, dv).astype(BF16)
+            for h, total in enumerate(line_sums(t, s, dv)):
+                line_out[t, s, h, dv] = total.astype(BF16)
                 line_copy(t, s, h, dv).start()
 
     def up_finish(t, s):
-        keep = []
+        keep = line_sums(t, s, 0)
+        blocks = line_in.at[t, s, :, pl.ds(0, 3)]
+        remote(blocks, blocks, p2_s.at[t, s], p2_r.at[t, s], sibling).wait_recv()
         for h in range(2):
-            total = line_sum(t, s, h, 0)
             for dv in (1, 3, 2):
-                line_copy(t, s, h, dv).wait_recv()
-                total = total + line_in[t, s, h, dv].astype(F32)
-            keep.append(total)
+                keep[h] = keep[h] + line_in[t, s, h, dv].astype(F32)
         residual_t = solved_t[2 - t, s] - jnp.concatenate(keep, axis=0)
         emit(2 - t, s, finish(2 - t, t + 1, s, residual_t))
 
@@ -413,17 +422,17 @@
     def drain(l, carry):
         for s in range(2):
             blocks = gath.at[l, s, pl.ds(0, 15)]
-            remote(blocks, blocks, ag_s.at[l, s], ag_r.at[l, s, 0, 0], sibling).wait_send()
+            remote(blocks, blocks, ag_s.at[l, s], ag_r.at[l, s, 0], sibling).wait_send()
             blocks = gath.at[l, s, pl.ds(0, 7)]
-            remote(blocks, blocks, col_s.at[l, s], col_r.at[l, s, 0, 0], sibling).wait_send()
+            remote(blocks, blocks, col_s.at[l, s], col_r.at[l, s], sibling).wait_send()
             blocks = part_out.at[l, s, :, pl.ds(0, 3)]
-            remote(blocks, blocks, p1_s.at[l, s], p1_r.at[l, s, 0, 0, 0], sibling).wait_send()
+            remote(blocks, blocks, p1_s.at[l, s], p1_r.at[l, s, 0], sibling).wait_send()
             blocks = line_out.at[l, s, :, pl.ds(0, 3)]
-            remote(blocks, blocks, p2_s.at[l, s], p2_r.at[l, s, 0, 0], sibling).wait_send()
+            remote(blocks, blocks, p2_s.at[l, s], p2_r.at[l, s], sibling).wait_send()
             blocks = upper.at[l, s, 0, pl.ds(0, 3)]
             remote(blocks, blocks, up_s.at[l, s], up_r.at[l, s, 0], sibling).wait_send()
             blocks = upper.at[l, s, 0]
-            remote(blocks, blocks, fw_s.at[l, s], fw_r.at[l, s, 0], sibling).wait_send()
+            remote(blocks, blocks, fw_s.at[l, s], fw_r.at[l, s], sibling).wait_send()
         return carry
 
     lax.fori_loop(0, 3, drain, 0)
@@ -457,6 +466,8 @@
             pltpu.VMEM((64, 1, B), F32),
             pltpu.VMEM((256, N), BF16),
             pltpu.VMEM((256, N), BF16),
+            pltpu.VMEM((512, 512), BF16),
+            pltpu.VMEM((2, 512, 256), BF16),
             pltpu.VMEM((NLEV, B, N), F32),
             pltpu.VMEM((3, 8, B, 16, B), BF16),
             pltpu.VMEM((3, 16, 2, 4, B, B), BF16),
@@ -471,9 +482,8 @@
             pltpu.VMEM((3, 2, 2, 4, H, B), BF16),
             pltpu.VMEM((3, 2, 2, 4, H, B), BF16),
             dma, dma, dma, dma, dma((2,)), dma((2,)),
-            dma((4,)), dma((3,)), dma((NLEV,)), dma((3, 2)), dma((3, 2, 2, 15)), dma((3, 2)), dma((3, 2, 2, 4)),
-            dma((3, 2)), dma((3, 2, 3)), dma((3, 2)), dma((3, 2, 4)),
-            dma((3, 2)), dma((3, 2, 2, 4, 4)), dma((3, 2)), dma((3, 2, 2, 4)),
+            dma((4,)), dma((3,)), dma((NLEV,)), dma((3, 2)), dma((3, 2, 8)), dma((3, 2)), dma((3, 2)),
+            dma((3, 2)), dma((3, 2, 3)), dma((3, 2)), dma((3, 2)), dma((3, 2)), dma((3, 2, 4)), dma((3, 2)), dma((3, 2)),
         ],
         compiler_params=pltpu.CompilerParams(
             collective_id=0, has_side_effects=True, vmem_limit_bytes=50 * 1024 * 1024

time: 118 us -> 115 us (0.975)
  Pallas kernels: 117 us -> 114 us
    pallas_call x1, Pallas kernels: 117 us -> 114 us  [solve(): pl.pallas_call(solve_kernel, out_shape=jax.ShapeDtypeStruct((NLEV, B, N),...]
where the time goes in v7:
time: 115 us
  Pallas kernels  114 us (99%)
    pallas_call x1, Pallas kernels, solve(): pl.pallas_call(solve_kernel, out_shape=jax.ShapeDtypeStruct((NLEV, B, N),...  114 us

profile of v7, /device:TPU:1, one launch (start us, length us, event | category | flops | bytes accessed | tf_op | source)
XLA Modules:
  0.0 114.5 jit_solution(12292395513610429298)
XLA Ops:
  0.0 113.8 %shard_map.55 = bf16[4,128,256]{2,1,0:T(8,128)(2,1)S(1)} custom-call(f32[512,256]{1,0:T(8,128)} %rhs_hbm.1, s32[1,512]{1,0:T(1,128)} %bitcast.7, bf16[4,128,128]{2,1,0:T(8,128)(2,1)} %bitcast.6, s32[3,1,8,1,16]{4,3,2,1,0:T(1,128)} %mask_hbm.1, bf16[3,1,8,128,1,16,128]{6,5,4,3,2,1,0:T(8,128)(2,1)} %w_hbm.1), custom_call_target="tpu_custom_call" | custom-call | tf_op jit(solution)/shard_map/pallas_call | solution.py:450
  113.8 0.7 copy.8

commit v8 on v7

--- a/solution.py
+++ b/solution.py
@@ -135,7 +135,6 @@
         pl.semaphore_signal(hello, inc=1, device_id=dev, device_id_type=MESH)
     for copy in inputs[2:]:
         copy.wait()
-    prepare(0, 0)
     pl.semaphore_wait(hello, 3)
 
     def send_rows(k, carry):
@@ -148,7 +147,7 @@
     rows_in[chip] = rows_out[chip]
     meta_in[chip] = meta_out[chip]
 
-    lax.fori_loop(1, 3, prepare, 0)
+    prepare(0, 0)
 
     some = pl.ds(0, 63)
     all_rows = remote(rows_out.at[some], rows_in.at[some], rows_s, rows_r, sibling)
@@ -357,12 +356,16 @@
     def top(s):
         emit(3, s, finish(3, 0, s, solved_t[3, s]))
 
-    for s in range(2):
-        set_solved(0, s, ordered_ref[0, :, s * C:(s + 1) * C].astype(BF16))
+    set_solved(0, 0, ordered_ref[0, :, :C].astype(BF16))
 
     def down(l, carry):
         down_send(l, 0)
 
+        @pl.when(l == 0)
+        def _():
+            set_solved(0, 1, ordered_ref[0, :, C:].astype(BF16))
+            prepare(1, 0)
+
         @pl.when(l > 0)
         def _():
             down_first(l - 1, 1)
@@ -375,6 +378,11 @@
             down_finish(l - 1, 1)
 
         down_send(l, 1)
+
+        @pl.when(l == 0)
+        def _():
+            prepare(2, 0)
+
         down_first(l, 0)
         down_second(l, 0)
         down_relay(l, 1)

time: 115 us -> 114 us (level)
    pallas_call x1, Pallas kernels: 114 us -> 113 us  [solve(): pl.pallas_call(solve_kernel, out_shape=jax.ShapeDtypeStruct((NLEV, B, N),...]
where the time goes in v8:
time: 114 us; the launch traced here: 113 us
  Pallas kernels  113 us (99%)
    pallas_call x1, Pallas kernels, solve(): pl.pallas_call(solve_kernel, out_shape=jax.ShapeDtypeStruct((NLEV, B, N),...  113 us

profile of v8, /device:TPU:1, one launch (start us, length us, event | category | flops | bytes accessed | tf_op | source)
XLA Modules:
  0.0 113.4 jit_solution(6521924322263309009)
XLA Ops:
  0.0 112.7 %shard_map.55 = bf16[4,128,256]{2,1,0:T(8,128)(2,1)S(1)} custom-call(f32[512,256]{1,0:T(8,128)} %rhs_hbm.1, s32[1,512]{1,0:T(1,128)} %bitcast.7, bf16[4,128,128]{2,1,0:T(8,128)(2,1)} %bitcast.6, s32[3,1,8,1,16]{4,3,2,1,0:T(1,128)} %mask_hbm.1, bf16[3,1,8,128,1,16,128]{6,5,4,3,2,1,0:T(8,128)(2,1)} %w_hbm.1), custom_call_target="tpu_custom_call" | custom-call | tf_op jit(solution)/shard_map/pallas_call | solution.py:458
  112.7 0.7 copy.8
